TPU v7x, 512 devices: a whole 4x4x16 slice. The times are simulated.
512 devices in a mesh: tok: 16 (over z), blk: 32 (over y, x, core).
Axes of the slice: x: 4, y: 4, z: 16, core: 2. Of those that a mesh axis runs over, the one named last changes fastest.
Arguments:
- acts: bfloat16 [2048, 8192], P('tok', 'blk'), may hold values from -35 to 35
- out_grad: bfloat16 [2048, 29568], P(('tok', 'blk')), may hold values from -0.12 to 0.12
- kept_ids: int32 [32, 16], replicated, may hold values from 0 to 14783, as said below
- cand_ids: int32 [32, 48], replicated, may hold values from 0 to 14783, as said below
Outputs:
- kept_grad: bfloat16 [32, 16, 128, 128], P('blk', 'tok')
- cand_score: float32 [32, 48], P('blk', 'tok')
Inputs may be any that keep to these rules, and one draw needn't show every extreme that they name: `kept_ids`: within one owner's kept and candidate blocks every block id appears once; one owner's blocks use at most 16 distinct block columns, exactly 16 for some owner, and no block column is used by two owners. `cand_ids`: numbered and owned as the kept blocks, and distinct from them.
All inputs are finite; a program needn't handle non-finite values.
Results may differ from a plain program's by a relative error of at most 0.001.
Values may be sent and summed in bfloat16 or wider, within the bound.
A program may use at most 64 MiB of HBM per device.

v0:
```python
import jax
import jax.numpy as jnp
from jax import lax
from jax.sharding import PartitionSpec as P

BLOCK = 128
KS = 16


def column_table(slot_cols, width):
    return jax.vmap(lambda cols: jnp.unique(cols, size=width, fill_value=0))(slot_cols).astype(
        jnp.int32
    )


def local(acts, out_grad, kept_ids, cand_ids):
    owners = lax.axis_size("blk")
    tok_count = lax.axis_size("tok")
    owner_index = lax.axis_index("blk")
    ncols = out_grad.shape[1] // BLOCK
    width = 2 * ((ncols + owners - 1) // owners)
    slot_ids = jnp.concatenate([kept_ids, cand_ids], axis=1)
    table = column_table(slot_ids % ncols, width)
    local_rows = out_grad.shape[0]
    grad3 = out_grad.reshape(local_rows, ncols, BLOCK)
    outgoing = jnp.take(grad3, table.reshape(-1), axis=1).reshape(local_rows, owners, width, BLOCK)
    incoming = lax.all_to_all(outgoing, "blk", split_axis=1, concat_axis=0, tiled=True)
    grad_cols = incoming.reshape(-1, width, BLOCK)
    acts_all = lax.all_gather(acts, "blk", axis=1, tiled=True)
    nrows = acts_all.shape[1] // BLOCK
    acts3 = acts_all.reshape(acts_all.shape[0], nrows, BLOCK)
    my_ids = lax.dynamic_index_in_dim(slot_ids, owner_index, 0, keepdims=False)
    my_table = lax.dynamic_index_in_dim(table, owner_index, 0, keepdims=False)
    row_index = my_ids // ncols
    matches = my_table[None, :] == (my_ids % ncols)[:, None]
    col_index = jnp.argmax(matches, axis=1)

    def one_group(indices):
        rows_here, cols_here = indices
        left = jnp.take(acts3, rows_here, axis=1)
        right = jnp.take(grad_cols, cols_here, axis=1)
        return jnp.einsum("tgi,tgj->gij", left, right, preferred_element_type=jnp.float32)

    total_slots = my_ids.shape[0]
    partials = lax.map(one_group, (row_index.reshape(-1, 16), col_index.reshape(-1, 16)))
    partials = partials.reshape(total_slots, BLOCK, BLOCK)
    kept_part = partials[:KS]
    cand_part = partials[KS:]
    kept_full, cand_full = lax.psum((kept_part, cand_part), "tok")
    tok_index = lax.axis_index("tok")
    kept_share = KS // tok_count
    cand_share = cand_part.shape[0] // tok_count
    kept_sum = lax.dynamic_slice_in_dim(kept_full, tok_index * kept_share, kept_share, 0)
    cand_sum = lax.dynamic_slice_in_dim(cand_full, tok_index * cand_share, cand_share, 0)
    kept_grad = kept_sum.astype(jnp.bfloat16)[None]
    norms = jnp.sqrt(jnp.sum(cand_sum * cand_sum, axis=(1, 2)))
    peak = lax.pmax(jnp.max(norms), ("tok", "blk"))
    cand_score = (norms / (peak + 1e-06))[None]
    return (kept_grad, cand_score)


def solution(mesh):
    return jax.shard_map(
        local,
        mesh=mesh,
        in_specs=(P("tok", "blk"), P(("tok", "blk"), None), P(), P()),
        out_specs=(P("blk", "tok", None, None), P("blk", "tok")),
        check_vma=False,
    )
```

profile of v0, /device:TPU:1, one launch (start us, length us, event | category | flops | bytes accessed | tf_op | source)
XLA Modules:
  0.0 373.8 jit_solution(273355379364645502)
XLA Ops:
  7.2 1.6 copy.111
  8.9 0.8 copy.110
  9.6 0.8 add_select_fusion.1
  10.5 1.0 sort.19
  11.6 1.0 copy.116
  13.4 13.6 %gather_fusion.3 = s32[2048]{0:T(1024)S(1)} fusion(s32[32,64]{1,0:T(8,128)S(1)} %add_select_fusion.1, s32[2048]{0:T(1024)S(1)} %reshape.347), kind=kCustom, calls=%fused_computation.3 | custom fusion | bytes 32768 | tf_op jit(solution)/shard_map/vmap(jit(_unique_sorted_mask))/gather | solution.py:11
  27.3 1.0 copy.118
  28.3 6.7 %compare_select_fusion.4 = s32[32,64,1]{2,0,1:T(8,128)S(1)} fusion(s32[32,64,1]{2,0,1:T(8,128)S(1)} %copy.118), kind=kOutput, calls=%fused_computation.28 | output fusion | flops 135168 | bytes 16384 | tf_op jit(solution)/shard_map/vmap(jit(cumsum))/reduce_window_sum | solution.py:11
  36.2 14.7 %scatter_custom_fusion = s32[512]{0:T(512)S(1)} fusion(s32[2048]{0:T(1024)S(1)} %reshape.359, s32[2048]{0:T(1024)S(1)} %broadcast.324, s32[]{:T(128)} %constant.169.clone.1), kind=kCustom, calls=%fused_computation.71 | custom fusion | flops 2048 | bytes 2052
  51.8 3.8 %gather_fusion.4 = s32[512]{0:T(512)S(1)} fusion(s32[32,64]{1,0:T(8,128)S(1)} %reshape.350, s32[512]{0:T(512)S(1)} %reshape.353), kind=kCustom, calls=%fused_computation.4 | custom fusion | bytes 8192 | tf_op jit(solution)/shard_map/vmap()/gather | solution.py:11
  55.9 2.1 gather_fusion.2
  58.2 0.9 copy.127
  59.1 10.4 %all-to-all-start = ((bf16[4,32,16,128]{3,2,0,1:T(8,128)(2,1)}), bf16[4,32,16,128]{3,2,0,1:T(8,128)(2,1)S(1)}, u32[]{:S(2)}, u32[]{:S(2)}) async-start(bf16[4,32,16,128]{3,2,0,1:T(8,128)(2,1)} %copy.127), calls=%async_computation | async-start | bytes 1048576 | tf_op jit(solution)/shard_map/all_to_all | solution.py:27
  70.6 10.7 %all-to-all-done = bf16[4,32,16,128]{3,2,0,1:T(8,128)(2,1)S(1)} async-done(((bf16[4,32,16,128]{3,2,0,1:T(8,128)(2,1)}), bf16[4,32,16,128]{3,2,0,1:T(8,128)(2,1)S(1)}, u32[]{:S(2)}, u32[]{:S(2)}) %all-to-all-start) | async-done | bytes 524320 | tf_op jit(solution)/shard_map/all_to_all | solution.py:27
  81.4 4.1 %copy.128 = bf16[128,64,128]{2,0,1:T(8,128)(2,1)} copy(bf16[128,64,128]{0,2,1:T(8,128)(2,1)} %bitcast.70) | data formatting | bytes 4194304 | tf_op jit(solution)/shard_map/while | solution.py:45
  85.5 17.5 %while.11 = (s32[]{:T(128)}, f32[4,16,128,128]{3,2,1,0:T(8,128)}, s32[4,16]{1,0:T(4,128)S(1)}, bf16[128,64,128]{2,0,1:T(8,128)(2,1)}, s32[4,16]{1,0:T(4,128)S(1)}, /*index=5*/bf16[128,16,128]{2,0,1:T(8,128)(2,1)S(1)}, s32[]{:T(128)}) while((s32[]{:T(128)}, f32[4,16,128,128]{3,2,1,0:T(8,128)}, s32[4,16]{1,0:T(4,128)S(1)}, ...), condition=%wide.region_7.8_spmd, body=%wide.region_6.7_spmd.sunk | while | flops 67635488 | bytes 4203797 | solution.py:45
  85.5 0.6 gather_fusion
  86.2 2.2 gather_fusion.1
  88.5 1.4 fusion.36
  89.9 0.6 gather_fusion
  90.6 2.2 gather_fusion.1
  92.8 1.5 fusion.36
  95.0 2.2 gather_fusion.1
  97.2 1.4 fusion.36
  99.3 2.2 gather_fusion.1
  101.6 1.4 fusion.36
  103.0 4.0 %slice.40 = f32[3,16,128,128]{3,2,1,0:T(8,128)} slice(f32[4,16,128,128]{3,2,1,0:T(8,128)} %get-tuple-element.50), slice={[1:4], [0:16], [0:128], [0:128]} | slice | bytes 6291456 | tf_op jit(solution)/shard_map/slice | solution.py:48
  107.0 1.3 slice_bitcast_fusion
  108.3 76.2 %all-reduce.5 = bf16[16,128,128]{2,1,0:T(8,128)(2,1)S(1)} all-reduce(f32[16,128,128]{2,1,0:T(8,128)S(1)} %slice_bitcast_fusion), channel_id=1, replica_groups=mesh['tok'=16,'blk'=32] {'tok'}, use_global_device_ids=true, to_apply=%region_8.9 | all-reduce | flops 262144 | bytes 1572864 | tf_op jit(solution)/shard_map/psum | solution.py:49
  184.5 69.3 %all-reduce.4.cloned.1.call-done = f32[48,128,128]{2,1,0:T(8,128)} async-done(((f32[48,128,128]{2,1,0:T(8,128)}), f32[48,128,128]{2,1,0:T(8,128)}) %all-reduce.4.cloned.1.call-update) | async-done | bytes 3145744 | tf_op jit(solution)/shard_map/psum | solution.py:49
  253.8 1.0 multiply_reduce_fusion
  256.1 109.7 %pmax.7 = f32[]{:T(128)} all-reduce(f32[]{:T(128)} %sqrt_reduce_fusion), channel_id=1, replica_groups=mesh['tok'=16,'blk'=32] {'tok','blk'}, use_global_device_ids=true, to_apply=%region_12.13 | all-reduce | flops 1 | bytes 8 | tf_op jit(solution)/shard_map/pmax | solution.py:57
  (78 shorter events, 8.2 us)
Async XLA Ops:
  7.2 48.7 %copy-start = (bf16[4,29568]{1,0:T(4,128)(2,1)S(1)}, bf16[4,29568]{1,0:T(4,128)(2,1)}, u32[]{:S(2)}) copy-start(bf16[4,29568]{1,0:T(4,128)(2,1)} %param.9) | copy-start | bytes 709636
  7.2 74.2 %all-gather.2.cloned.1.call-start = ((), (), s32[]{:S(2)}) async-start(), calls=%async_computation.1 | async-start | bytes 2162688 | tf_op jit(solution)/shard_map/all_gather | solution.py:29
  27.1 8.6 %copy-start.2 = (s32[2]{0:T(128)S(1)}, s32[2]{0:T(128)}, u32[]{:S(2)}) copy-start(s32[2]{0:T(128)} %constant.192) | copy-start | bytes 28
  27.1 8.7 %copy-start.3 = (s32[2]{0:T(128)S(1)}, s32[2]{0:T(128)}, u32[]{:S(2)}) copy-start(s32[2]{0:T(128)} %constant.195) | copy-start | bytes 28
  55.6 13.9 %copy-start.1 = (s32[32,48]{1,0:T(8,128)S(1)}, s32[32,48]{1,0:T(8,128)}, u32[]{:S(2)}) copy-start(s32[32,48]{1,0:T(8,128)} %param.11) | copy-start | bytes 18436
  59.1 22.2 %all-to-all-start = ((bf16[4,32,16,128]{3,2,0,1:T(8,128)(2,1)}), bf16[4,32,16,128]{3,2,0,1:T(8,128)(2,1)S(1)}, u32[]{:S(2)}, u32[]{:S(2)}) async-start(bf16[4,32,16,128]{3,2,0,1:T(8,128)(2,1)} %copy.127), calls=%async_computation | async-start | bytes 1048576 | tf_op jit(solution)/shard_map/all_to_all | solution.py:27
  69.5 184.3 %all-reduce.4.cloned.1.call-start = ((), (), s32[]{:S(2)}) async-start(), calls=%async_computation.2 | async-start | bytes 6291456 | tf_op jit(solution)/shard_map/psum | solution.py:49
Sparse Core Ops, SparseCore 0:
  11.1 66.0 all-gather.1
  107.1 146.6 all-reduce.3
where the time goes:
time: 374 us
  blocking collectives  186 us (50%)
  waiting for transfers between devices  80 us (21%)
  local copies, waits for them, and re-layouts  49.3 us (13%)
  other arithmetic  27.4 us (7%)
  between operations  14.9 us (4%)
  starting transfers between devices  10.5 us (3%)
  matrix products  5.7 us (2%)
    pmax x1, blocking collectives, local(): peak = lax.pmax(jnp.max(norms), ('tok', 'blk'))  110 us
    psum x1, blocking collectives, local(): kept_full, cand_full = lax.psum((kept_part, cand_part), 'tok')  76.2 us
    psum x1, waiting for transfers between devices, local(): kept_full, cand_full = lax.psum((kept_part, cand_part), 'tok')  69.3 us
    gather x9, local copies, waits for them, and re-layouts, column_table(): jnp.unique(cols, size=width, fill_value=0)  19.6 us
    unnamed x4, other arithmetic  14.8 us
    all_to_all x1, waiting for transfers between devices, local(): lax.all_to_all(outgoing, 'blk', split_axis=1, concat_axis=0, tiled=True)  10.7 us
    all_to_all x1, starting transfers between devices, local(): lax.all_to_all(outgoing, 'blk', split_axis=1, concat_axis=0, tiled=True)  10.4 us
    gather x4, local copies, waits for them, and re-layouts, one_group(): left = jnp.take(acts3, rows_here, axis=1)  8.96 us
  transfers between devices with their start and end apart: 3, of which 2 were waited for; matrix products, arithmetic and copies ran while one was open for 14% of the time, Pallas kernels for 0%

commit v1 on v0

v1 whole, which is shorter than its diff:
```python
import jax
import jax.numpy as jnp
from jax import lax
from jax.experimental import pallas as pl
from jax.experimental.pallas import tpu as pltpu
from jax.sharding import PartitionSpec as P

BLOCK = 128
KS = 16


def column_tables(cols, width):
    slots = cols.shape[1]
    same = cols[:, :, None] == cols[:, None, :]
    place = jnp.arange(slots)
    earlier = place[None, :] < place[:, None]
    first = jnp.logical_not(jnp.any(same & earlier[None], axis=2))
    rank = jnp.sum(jnp.where(earlier[None] & first[:, None, :], 1, 0), axis=2)
    position = jnp.sum(jnp.where(same & first[:, None, :], rank[:, None, :], 0), axis=2)
    hit = first[:, None, :] & (rank[:, None, :] == jnp.arange(width)[None, :, None])
    table = jnp.sum(jnp.where(hit, cols[:, None, :], 0), axis=2)
    return table.astype(jnp.int32), position.astype(jnp.int32)


def pick_kernel(owners, width, table_ref, grad_ref, out_ref):
    def one_owner(o, carry):
        for w in range(width):
            col = table_ref[o * width + w]
            out_ref[o, :, w * BLOCK : (w + 1) * BLOCK] = grad_ref[
                :, pl.ds(pl.multiple_of(col * BLOCK, BLOCK), BLOCK)
            ]
        return carry

    lax.fori_loop(0, owners, one_owner, 0)


def product_kernel(per, rows_ref, cols_ref, acts_ref, grad_ref, kept_ref, cand_ref):
    def product(slot):
        row = rows_ref[slot]
        col = cols_ref[slot]
        left = acts_ref[row // per, :, pl.ds(pl.multiple_of((row % per) * BLOCK, BLOCK), BLOCK)]
        right = grad_ref[:, pl.ds(pl.multiple_of(col * BLOCK, BLOCK), BLOCK)]
        return lax.dot_general(
            left, right, (((0,), (0,)), ((), ())), preferred_element_type=jnp.float32
        )

    def kept(j, carry):
        for u in range(4):
            kept_ref[4 * j + u] = product(4 * j + u)
        return carry

    def cand(j, carry):
        for u in range(4):
            cand_ref[4 * j + u] = product(kept_ref.shape[0] + 4 * j + u).astype(cand_ref.dtype)
        return carry

    lax.fori_loop(0, kept_ref.shape[0] // 4, kept, 0)
    lax.fori_loop(0, cand_ref.shape[0] // 4, cand, 0)


def score_kernel(norm_ref, score_ref, line, plane, own_sem, line_send, line_recv, plane_send, plane_recv):
    nt, nb = lax.axis_size("tok"), lax.axis_size("blk")
    t, b = lax.axis_index("tok"), lax.axis_index("blk")
    barrier = pltpu.get_barrier_semaphore()

    def greet(axis, me, n):
        def one(k, carry):
            pl.semaphore_signal(
                barrier, inc=1, device_id={axis: lax.rem(me + k, n)}, device_id_type=pl.DeviceIdType.MESH
            )
            return carry

        lax.fori_loop(1, n, one, 0)

    greet("tok", t, nt)
    greet("blk", b, nb)
    pl.semaphore_wait(barrier, nt + nb - 2)

    def exchange(axis, me, n, src, buf, send, recv):
        def copy(k, slot):
            return pltpu.make_async_remote_copy(
                src_ref=src,
                dst_ref=buf.at[slot],
                send_sem=send.at[k],
                recv_sem=recv.at[k],
                device_id={axis: lax.rem(me + k, n)},
                device_id_type=pl.DeviceIdType.MESH,
            )

        def start(k, carry):
            copy(k, me).start()
            return carry

        def finish(k, carry):
            arrived = copy(k, lax.rem(me + n - k, n))
            arrived.wait_send()
            arrived.wait_recv()
            return carry

        lax.fori_loop(1, n, start, 0)
        own = pltpu.make_async_copy(src, buf.at[me], own_sem)
        own.start()
        own.wait()
        lax.fori_loop(1, n, finish, 0)

    exchange("tok", t, nt, norm_ref, line, line_send, line_recv)
    exchange("blk", b, nb, line, plane, plane_send, plane_recv)
    peak = jnp.max(plane[...])
    score_ref[...] = norm_ref[...] / (peak + 1e-06)


def local(acts, out_grad, kept_ids, cand_ids):
    owners = lax.axis_size("blk")
    owner_index = lax.axis_index("blk")
    ncols = out_grad.shape[1] // BLOCK
    width = 2 * ((ncols + owners - 1) // owners)
    tokens = acts.shape[0]
    per = acts.shape[1] // BLOCK
    slot_ids = jnp.concatenate([kept_ids, cand_ids], axis=1)
    acts_all = lax.all_gather(acts, "blk", axis=0, tiled=False)
    table, position = column_tables(slot_ids % ncols, width)
    vmem = pl.BlockSpec(memory_space=pltpu.VMEM)
    smem = pl.BlockSpec(memory_space=pltpu.SMEM)
    outgoing = pl.pallas_call(
        lambda *refs: pick_kernel(owners, width, *refs),
        out_shape=jax.ShapeDtypeStruct((owners, out_grad.shape[0], width * BLOCK), out_grad.dtype),
        in_specs=[smem, vmem],
        out_specs=vmem,
        name="pick",
    )(table.reshape(-1), out_grad)
    incoming = lax.all_to_all(outgoing, "blk", split_axis=0, concat_axis=0, tiled=True)
    grad_cols = incoming.reshape(tokens, width * BLOCK)
    my_rows = lax.dynamic_index_in_dim(slot_ids // ncols, owner_index, 0, keepdims=False)
    my_cols = lax.dynamic_index_in_dim(position, owner_index, 0, keepdims=False)
    kept_part, cand_part = pl.pallas_call(
        lambda *refs: product_kernel(per, *refs),
        out_shape=(
            jax.ShapeDtypeStruct((KS, BLOCK, BLOCK), jnp.float32),
            jax.ShapeDtypeStruct((cand_ids.shape[1], BLOCK, BLOCK), jnp.bfloat16),
        ),
        in_specs=[smem, smem, vmem, vmem],
        out_specs=(vmem, vmem),
        name="products",
    )(my_rows, my_cols, acts_all, grad_cols)
    cand_sum = lax.psum_scatter(cand_part, "tok", scatter_dimension=0, tiled=True)
    kept_sum = lax.psum_scatter(kept_part, "tok", scatter_dimension=0, tiled=True)
    kept_grad = kept_sum.astype(jnp.bfloat16)[None]
    cand_sum = cand_sum.astype(jnp.float32)
    norms = jnp.sqrt(jnp.sum(cand_sum * cand_sum, axis=(1, 2)))
    toks = lax.axis_size("tok")
    share = norms.shape[0]
    dma = pltpu.SemaphoreType.DMA
    scores = pl.pallas_call(
        score_kernel,
        out_shape=jax.ShapeDtypeStruct((1, BLOCK), jnp.float32),
        in_specs=[vmem],
        out_specs=vmem,
        scratch_shapes=[
            pltpu.VMEM((toks, 1, BLOCK), jnp.float32),
            pltpu.VMEM((owners, toks, 1, BLOCK), jnp.float32),
            dma,
            dma((toks,)),
            dma((toks,)),
            dma((owners,)),
            dma((owners,)),
        ],
        compiler_params=pltpu.CompilerParams(collective_id=0, has_side_effects=True),
        name="scores",
    )(jnp.pad(norms, (0, BLOCK - share))[None])
    cand_score = scores[:, :share]
    return (kept_grad, cand_score)


def solution(mesh):
    return jax.shard_map(
        local,
        mesh=mesh,
        in_specs=(P("tok", "blk"), P(("tok", "blk"), None), P(), P()),
        out_specs=(P("blk", "tok", None, None), P("blk", "tok")),
        check_vma=False,
    )
```

time: 374 us -> 259 us (0.69)
  blocking collectives: 186 us -> 0 us
  waiting for transfers between devices: 80 us -> 180 us
  local copies, waits for them, and re-layouts: 49.3 us -> 4.1 us
  Pallas kernels: 0 us -> 43.1 us
  other arithmetic: 27.4 us -> 7.14 us
  matrix products: 5.7 us -> 0 us
    reduce_scatter x0 -> x2, waiting for transfers between devices: none -> 131 us  [the longest x1 71.7 us: local(): lax.psum_scatter(cand_part, 'tok', scatter_dimension=0, tiled=True)]
    pmax x1 -> x0, blocking collectives: 110 us -> none  [local(): peak = lax.pmax(jnp.max(norms), ('tok', 'blk'))]
    psum x1 -> x0, blocking collectives: 76.2 us -> none  [local(): kept_full, cand_full = lax.psum((kept_part, cand_part), 'tok')]
    psum x1 -> x0, waiting for transfers between devices: 69.3 us -> none  [local(): kept_full, cand_full = lax.psum((kept_part, cand_part), 'tok')]
    pallas_call x0 -> x3, Pallas kernels: none -> 43.1 us  [the longest x1 33.7 us: local(): pl.pallas_call(score_kernel, out_shape=jax.ShapeDtypeStruct((1, BLOCK), j...]
    all_gather x1, waiting for transfers between devices: 0.02 us -> 37.8 us  [local(): acts_all = lax.all_gather(acts, 'blk', axis=0, tiled=False)]
    gather x19 -> x0, local copies, waits for them, and re-layouts: 33.3 us -> none  [the longest x9 19.6 us: column_table(): jnp.unique(cols, size=width, fill_value=0)]
    unnamed x4 -> x0, other arithmetic: 14.8 us -> none
  transfers between devices with their start and end apart: 3 -> 4, of which waited for: 2 -> 4; matrix products, arithmetic and copies ran while one was open for 14% -> 3% of each run, Pallas kernels for 0% -> 1%
where the time goes in v1:
time: 259 us
  waiting for transfers between devices  180 us (69%)
  Pallas kernels  43.1 us (17%)
  between operations  13.8 us (5%)
  starting transfers between devices  10.5 us (4%)
  other arithmetic  7.14 us (3%)
  local copies, waits for them, and re-layouts  4.1 us (2%)
    reduce_scatter x1, waiting for transfers between devices, local(): lax.psum_scatter(cand_part, 'tok', scatter_dimension=0, tiled=True)  71.7 us
    reduce_scatter x1, waiting for transfers between devices, local(): lax.psum_scatter(kept_part, 'tok', scatter_dimension=0, tiled=True)  59.5 us
    all_gather x1, waiting for transfers between devices, local(): acts_all = lax.all_gather(acts, 'blk', axis=0, tiled=False)  37.8 us
    pallas_call x1, Pallas kernels, local(): pl.pallas_call(score_kernel, out_shape=jax.ShapeDtypeStruct((1, BLOCK), j...  33.7 us
    all_to_all x1, starting transfers between devices, local(): lax.all_to_all(outgoing, 'blk', split_axis=0, concat_axis=0, tiled=True)  10.4 us
    all_to_all x1, waiting for transfers between devices, local(): lax.all_to_all(outgoing, 'blk', split_axis=0, concat_axis=0, tiled=True)  9.82 us
    pallas_call x1, Pallas kernels, local(): pl.pallas_call(lambda *refs: product_kernel(per, *refs), out_shape=(jax.S...  6.67 us
  transfers between devices with their start and end apart: 4, of which 4 were waited for; matrix products, arithmetic and copies ran while one was open for 3% of the time, Pallas kernels for 1%

profile of v1, /device:TPU:1, one launch (start us, length us, event | category | flops | bytes accessed | tf_op | source)
XLA Modules:
  0.0 258.8 jit_solution(15295244543809924262)
XLA Ops:
  7.2 0.0 copy-start
  7.2 0.0 all-gather.3.cloned.1.call-start
  7.2 0.7 all-gather.3.cloned.1.call-update
  7.9 0.8 copy.8
  8.7 0.8 add_select_fusion
  9.5 0.9 fusion
  10.5 0.6 select_reduce_fusion.1
  11.1 0.6 select_reduce_fusion.2
  11.7 0.7 reshape.66.refs_0_
  12.4 2.7 %pick.1 = bf16[32,4,2048]{2,1,0:T(4,128)(2,1)} custom-call(s32[512]{0:T(512)} %reshape.66.refs_0_, bf16[4,29568]{1,0:T(4,128)(2,1)} %refs_1_.1), custom_call_target="tpu_custom_call" | custom-call | tf_op jit(solution)/shard_map/pick/pallas_call | solution.py:124
  15.1 10.4 %all-to-all-start = ((bf16[32,4,2048]{2,1,0:T(4,128)(2,1)}), bf16[32,4,2048]{2,1,0:T(4,128)(2,1)S(1)}, u32[]{:S(2)}, u32[]{:S(2)}) async-start(bf16[32,4,2048]{2,1,0:T(4,128)(2,1)} %pick.1), calls=%async_computation | async-start | bytes 1048576 | tf_op jit(solution)/shard_map/all_to_all | solution.py:131
  25.5 0.0 reduce-scatter.3.cloned.1.call-start
  25.5 0.0 copy-done
  25.5 0.1 broadcast_compare_fusion
  25.6 1.0 select_reduce_fusion
  26.6 0.6 fusion.3
  27.2 9.8 %all-to-all-done = bf16[32,4,2048]{2,1,0:T(4,128)(2,1)S(1)} async-done(((bf16[32,4,2048]{2,1,0:T(4,128)(2,1)}), bf16[32,4,2048]{2,1,0:T(4,128)(2,1)S(1)}, u32[]{:S(2)}, u32[]{:S(2)}) %all-to-all-start) | async-done | bytes 524320 | tf_op jit(solution)/shard_map/all_to_all | solution.py:131
  37.0 0.9 reshape.67.refs_3_
  38.0 37.8 %all-gather.3.cloned.1.call-done = bf16[4096,256]{1,0:T(8,128)(2,1)} async-done(((bf16[128,256]{1,0:T(8,128)(2,1)}), bf16[4096,256]{1,0:T(8,128)(2,1)}) %all-gather.3.cloned.1.call-update) | async-done | bytes 2097168 | tf_op jit(solution)/shard_map/all_gather | solution.py:120
  75.7 6.7 %products.1 = (f32[16,128,128]{2,1,0:T(8,128)}, bf16[48,128,128]{2,1,0:T(8,128)(2,1)}) custom-call(s32[64]{0:T(128)} %get-tuple-element.7.refs_0_, s32[64]{0:T(128)} %get-tuple-element.6.refs_1_, bf16[32,128,256]{2,1,0:T(8,128)(2,1)} %bitcast.10, bf16[128,2048]{1,0:T(8,128)(2,1)} %reshape.67.refs_3_), custom_call_target="tpu_custom_call" | custom-call | tf_op jit(solution)/shard_map/products/pallas_call | solution.py:135
  82.4 0.0 reduce-scatter.3.cloned.1.call-update
  82.4 0.0 reduce-scatter.5.cloned.1.call-start
  82.5 0.7 reduce-scatter.5.cloned.1.call-update
  83.2 59.5 %reduce-scatter.3.cloned.1.call-done = f32[1,128,128]{2,1,0:T(8,128)} async-done(((f32[16,128,128]{2,1,0:T(8,128)}), f32[1,128,128]{2,1,0:T(8,128)}) %reduce-scatter.3.cloned.1.call-update) | async-done | bytes 65552 | tf_op jit(solution)/shard_map/reduce_scatter | solution.py:146
  142.6 1.5 convert_bitcast_fusion
  144.1 71.7 %reduce-scatter.5.cloned.1.call-done = bf16[3,128,128]{2,1,0:T(8,128)(2,1)} async-done(((bf16[48,128,128]{2,1,0:T(8,128)(2,1)}), bf16[3,128,128]{2,1,0:T(8,128)(2,1)}) %reduce-scatter.5.cloned.1.call-update) | async-done | bytes 98320 | tf_op jit(solution)/shard_map/reduce_scatter | solution.py:145
  215.8 1.0 multiply_reduce_fusion
  216.8 0.5 pad_bitcast_fusion.norm_ref
  217.4 33.7 %scores.1 = f32[1,128]{1,0:T(1,128)} custom-call(f32[1,128]{1,0:T(1,128)} %pad_bitcast_fusion.norm_ref), custom_call_target="tpu_custom_call" | custom-call | tf_op jit(solution)/shard_map/scores/pallas_call | solution.py:153
  251.1 1.2 copy.10
  (3 shorter events, 0.0 us)
Async XLA Ops:
  7.2 18.4 %copy-start = (s32[32,48]{1,0:T(8,128)S(1)}, s32[32,48]{1,0:T(8,128)}, u32[]{:S(2)}) copy-start(s32[32,48]{1,0:T(8,128)} %param.7) | copy-start | bytes 18436
  7.2 68.5 %all-gather.3.cloned.1.call-start = ((), (), s32[]{:S(2)}) async-start(), calls=%async_computation.5 | async-start | bytes 2162688 | tf_op jit(solution)/shard_map/all_gather | solution.py:120
  15.1 21.9 %all-to-all-start = ((bf16[32,4,2048]{2,1,0:T(4,128)(2,1)}), bf16[32,4,2048]{2,1,0:T(4,128)(2,1)S(1)}, u32[]{:S(2)}, u32[]{:S(2)}) async-start(bf16[32,4,2048]{2,1,0:T(4,128)(2,1)} %pick.1), calls=%async_computation | async-start | bytes 1048576 | tf_op jit(solution)/shard_map/all_to_all | solution.py:131
  25.5 117.2 %reduce-scatter.3.cloned.1.call-start = ((), (), s32[]{:S(2)}) async-start(), calls=%async_computation.3 | async-start | bytes 1114112 | tf_op jit(solution)/shard_map/reduce_scatter | solution.py:146
  82.4 133.4 %reduce-scatter.5.cloned.1.call-start = ((), (), s32[]{:S(2)}) async-start(), calls=%async_computation.4 | async-start | bytes 1671168 | tf_op jit(solution)/shard_map/reduce_scatter | solution.py:145
Sparse Core Ops, SparseCore 0:
  11.1 64.5 all-gather.2
  82.5 60.0 reduce-scatter.2
  145.5 70.3 reduce-scatter.4

commit v2 on v1

--- a/solution.py
+++ b/solution.py
@@ -58,55 +58,148 @@
     lax.fori_loop(0, cand_ref.shape[0] // 4, cand, 0)
 
 
-def score_kernel(norm_ref, score_ref, line, plane, own_sem, line_send, line_recv, plane_send, plane_recv):
+MESH = pl.DeviceIdType.MESH
+
+
+def greet(barrier, axis, me, n):
+    def one(k, carry):
+        pl.semaphore_signal(
+            barrier, inc=1, device_id={axis: lax.rem(me + k, n)}, device_id_type=MESH
+        )
+        return carry
+
+    lax.fori_loop(1, n, one, 0)
+
+
+def exchange(axis, me, n, src, buf, send, recv, own_sem):
+    def copy(k, slot):
+        return pltpu.make_async_remote_copy(
+            src_ref=src,
+            dst_ref=buf.at[slot],
+            send_sem=send.at[k],
+            recv_sem=recv.at[k],
+            device_id={axis: lax.rem(me + k, n)},
+            device_id_type=MESH,
+        )
+
+    def start(k, carry):
+        copy(k, me).start()
+        return carry
+
+    def finish(k, carry):
+        arrived = copy(k, lax.rem(me + n - k, n))
+        arrived.wait_send()
+        arrived.wait_recv()
+        return carry
+
+    lax.fori_loop(1, n, start, 0)
+    own = pltpu.make_async_copy(src, buf.at[me], own_sem)
+    own.start()
+    own.wait()
+    lax.fori_loop(1, n, finish, 0)
+
+
+def update_kernel(
+    kept_part, cand_part, kept_ref, score_ref,
+    kept_buf, cand_buf, send_sems, recv_sems,
+    norm_buf, mine, line, plane, own_sem, line_send, line_recv, plane_send, plane_recv,
+):
     nt, nb = lax.axis_size("tok"), lax.axis_size("blk")
     t, b = lax.axis_index("tok"), lax.axis_index("blk")
+    kshare, cshare = kept_buf.shape[2], cand_buf.shape[2]
+    blocks = kshare + cshare
+    up_hops = nt // 2
+    down_hops = nt - 1 - up_hops
+    hops = (up_hops, down_hops)
+    peers = (lax.rem(t + 1, nt), lax.rem(t + nt - 1, nt))
+
     barrier = pltpu.get_barrier_semaphore()
-
-    def greet(axis, me, n):
-        def one(k, carry):
-            pl.semaphore_signal(
-                barrier, inc=1, device_id={axis: lax.rem(me + k, n)}, device_id_type=pl.DeviceIdType.MESH
-            )
-            return carry
-
-        lax.fori_loop(1, n, one, 0)
-
-    greet("tok", t, nt)
-    greet("blk", b, nb)
+    greet(barrier, "tok", t, nt)
+    greet(barrier, "blk", b, nb)
+
+    def product(d, j):
+        if j < kshare:
+            return kept_part[d * kshare + j]
+        return cand_part[d * cshare + (j - kshare)].astype(jnp.float32)
+
+    def home(way, step):
+        if way == 0:
+            return lax.rem(t + up_hops - step + nt, nt)
+        return lax.rem(t + nt - down_hops + step, nt)
+
+    def block(way, step, j):
+        if j < kshare:
+            return kept_buf.at[way, step, j]
+        return cand_buf.at[way, step, j - kshare]
+
+    def copy(way, step, j):
+        return pltpu.make_async_remote_copy(
+            src_ref=block(way, step, j),
+            dst_ref=block(way, step + 1, j),
+            send_sem=send_sems.at[way, step, j],
+            recv_sem=recv_sems.at[way, step, j],
+            device_id={"tok": peers[way]},
+            device_id_type=MESH,
+        )
+
+    def advance(way, step, j):
+        term = product(home(way, step), j)
+        copy(way, step - 1, j).wait_recv()
+        here = block(way, step, j)
+        here[...] = (here[...].astype(jnp.float32) + term).astype(here.dtype)
+        copy(way, step, j).start()
+
+    for way in range(2):
+        for j in range(blocks):
+            here = block(way, 0, j)
+            here[...] = product(home(way, 0), j).astype(here.dtype)
     pl.semaphore_wait(barrier, nt + nb - 2)
-
-    def exchange(axis, me, n, src, buf, send, recv):
-        def copy(k, slot):
-            return pltpu.make_async_remote_copy(
-                src_ref=src,
-                dst_ref=buf.at[slot],
-                send_sem=send.at[k],
-                recv_sem=recv.at[k],
-                device_id={axis: lax.rem(me + k, n)},
-                device_id_type=pl.DeviceIdType.MESH,
-            )
-
-        def start(k, carry):
-            copy(k, me).start()
-            return carry
-
-        def finish(k, carry):
-            arrived = copy(k, lax.rem(me + n - k, n))
-            arrived.wait_send()
-            arrived.wait_recv()
-            return carry
-
-        lax.fori_loop(1, n, start, 0)
-        own = pltpu.make_async_copy(src, buf.at[me], own_sem)
-        own.start()
-        own.wait()
-        lax.fori_loop(1, n, finish, 0)
-
-    exchange("tok", t, nt, norm_ref, line, line_send, line_recv)
-    exchange("blk", b, nb, line, plane, plane_send, plane_recv)
-    peak = jnp.max(plane[...])
-    score_ref[...] = norm_ref[...] / (peak + 1e-06)
+    for j in range(blocks):
+        for way in range(2):
+            copy(way, 0, j).start()
+
+    def both(step, carry):
+        for j in range(blocks):
+            for way in range(2):
+                advance(way, step, j)
+        return carry
+
+    lax.fori_loop(1, down_hops, both, 0)
+    for step in range(down_hops, up_hops):
+        for j in range(blocks):
+            advance(0, step, j)
+
+    lane = lax.broadcasted_iota(jnp.int32, norm_buf.shape, 1)
+    squares = jnp.zeros(norm_buf.shape, jnp.float32)
+    for j in range(blocks):
+        total = product(t, j)
+        for way in (1, 0):
+            copy(way, hops[way] - 1, j).wait_recv()
+            total = total + block(way, hops[way], j)[...].astype(jnp.float32)
+        if j < kshare:
+            kept_ref[j] = total.astype(kept_ref.dtype)
+        else:
+            squares = jnp.where(lane == j - kshare, jnp.sum(total * total), squares)
+    norms = jnp.sqrt(squares)
+    norm_buf[...] = norms
+    own = pltpu.make_async_copy(norm_buf, mine, own_sem)
+    own.start()
+
+    def sent(step, carry):
+        for way in range(2):
+            for j in range(blocks):
+                copy(way, step, j).wait_send()
+        return carry
+
+    lax.fori_loop(0, down_hops, sent, 0)
+    for step in range(down_hops, up_hops):
+        for j in range(blocks):
+            copy(0, step, j).wait_send()
+    own.wait()
+
+    exchange("tok", t, nt, mine, line, line_send, line_recv, own_sem)
+    exchange("blk", b, nb, line, plane, plane_send, plane_recv, own_sem)
+    score_ref[...] = norms / (jnp.max(plane[...]) + 1e-06)
 
 
 def local(acts, out_grad, kept_ids, cand_ids):
@@ -142,20 +235,25 @@
         out_specs=(vmem, vmem),
         name="products",
     )(my_rows, my_cols, acts_all, grad_cols)
-    cand_sum = lax.psum_scatter(cand_part, "tok", scatter_dimension=0, tiled=True)
-    kept_sum = lax.psum_scatter(kept_part, "tok", scatter_dimension=0, tiled=True)
-    kept_grad = kept_sum.astype(jnp.bfloat16)[None]
-    cand_sum = cand_sum.astype(jnp.float32)
-    norms = jnp.sqrt(jnp.sum(cand_sum * cand_sum, axis=(1, 2)))
     toks = lax.axis_size("tok")
-    share = norms.shape[0]
+    kshare, share = KS // toks, cand_ids.shape[1] // toks
+    steps = toks // 2
     dma = pltpu.SemaphoreType.DMA
-    scores = pl.pallas_call(
-        score_kernel,
-        out_shape=jax.ShapeDtypeStruct((1, BLOCK), jnp.float32),
-        in_specs=[vmem],
-        out_specs=vmem,
+    kept_grad, scores = pl.pallas_call(
+        update_kernel,
+        out_shape=(
+            jax.ShapeDtypeStruct((kshare, BLOCK, BLOCK), jnp.bfloat16),
+            jax.ShapeDtypeStruct((1, BLOCK), jnp.float32),
+        ),
+        in_specs=[vmem, vmem],
+        out_specs=(vmem, vmem),
         scratch_shapes=[
+            pltpu.VMEM((2, steps + 1, kshare, BLOCK, BLOCK), jnp.float32),
+            pltpu.VMEM((2, steps + 1, share, BLOCK, BLOCK), jnp.bfloat16),
+            dma((2, steps, kshare + share)),
+            dma((2, steps, kshare + share)),
+            pltpu.VMEM((1, BLOCK), jnp.float32),
+            pltpu.VMEM((1, BLOCK), jnp.float32),
             pltpu.VMEM((toks, 1, BLOCK), jnp.float32),
             pltpu.VMEM((owners, toks, 1, BLOCK), jnp.float32),
             dma,
@@ -165,10 +263,10 @@
             dma((owners,)),
         ],
         compiler_params=pltpu.CompilerParams(collective_id=0, has_side_effects=True),
-        name="scores",
-    )(jnp.pad(norms, (0, BLOCK - share))[None])
+        name="update",
+    )(kept_part, cand_part)
     cand_score = scores[:, :share]
-    return (kept_grad, cand_score)
+    return (kept_grad[None], cand_score)
 
 
 def solution(mesh):

time: 259 us -> 151 us (0.58)
  waiting for transfers between devices: 180 us -> 48.3 us
  Pallas kernels: 43.1 us -> 68.3 us
    reduce_scatter x2 -> x0, waiting for transfers between devices: 131 us -> none  [the longest x1 71.7 us: local(): lax.psum_scatter(cand_part, 'tok', scatter_dimension=0, tiled=True)]
    pallas_call x1, Pallas kernels: 33.7 us -> 58.9 us  [local(): pl.pallas_call(update_kernel, out_shape=(jax.ShapeDtypeStruct((kshare, BL...]
  transfers between devices with their start and end apart: 4 -> 2, of which waited for: 4 -> 2; matrix products, arithmetic and copies ran while one was open for 3% -> 5% of each run, Pallas kernels for 1% -> 2%
where the time goes in v2:
time: 151 us
  Pallas kernels  68.3 us (45%)
  waiting for transfers between devices  48.3 us (32%)
  between operations  14.1 us (9%)
  starting transfers between devices  10.4 us (7%)
  local copies, waits for them, and re-layouts  4.9 us (3%)
  other arithmetic  4.66 us (3%)
    pallas_call x1, Pallas kernels, local(): pl.pallas_call(update_kernel, out_shape=(jax.ShapeDtypeStruct((kshare, BL...  58.9 us
    all_gather x1, waiting for transfers between devices, local(): acts_all = lax.all_gather(acts, 'blk', axis=0, tiled=False)  37.8 us
    all_to_all x1, starting transfers between devices, local(): lax.all_to_all(outgoing, 'blk', split_axis=0, concat_axis=0, tiled=True)  10.4 us
    all_to_all x1, waiting for transfers between devices, local(): lax.all_to_all(outgoing, 'blk', split_axis=0, concat_axis=0, tiled=True)  9.87 us
    pallas_call x1, Pallas kernels, local(): pl.pallas_call(lambda *refs: product_kernel(per, *refs), out_shape=(jax.S...  6.67 us
    unnamed x5, local copies, waits for them, and re-layouts  3.29 us
  transfers between devices with their start and end apart: 2, of which 2 were waited for; matrix products, arithmetic and copies ran while one was open for 5% of the time, Pallas kernels for 2%

profile of v2, /device:TPU:1, one launch (start us, length us, event | category | flops | bytes accessed | tf_op | source)
XLA Modules:
  0.0 150.7 jit_solution(13967711350959306567)
XLA Ops:
  7.2 0.0 copy-start
  7.2 0.0 all-gather.3.cloned.1.call-start
  7.2 0.7 all-gather.3.cloned.1.call-update
  7.9 0.8 copy.8
  8.7 0.8 add_select_fusion
  9.5 0.9 fusion
  10.5 0.6 select_reduce_fusion.1
  11.1 0.6 select_reduce_fusion.2
  11.7 0.7 reshape.66.refs_0_
  12.4 2.7 %pick.1 = bf16[32,4,2048]{2,1,0:T(4,128)(2,1)} custom-call(s32[512]{0:T(512)} %reshape.66.refs_0_, bf16[4,29568]{1,0:T(4,128)(2,1)} %refs_1_.1), custom_call_target="tpu_custom_call" | custom-call | tf_op jit(solution)/shard_map/pick/pallas_call | solution.py:217
  15.1 10.4 %all-to-all-start = ((bf16[32,4,2048]{2,1,0:T(4,128)(2,1)}), bf16[32,4,2048]{2,1,0:T(4,128)(2,1)S(1)}, u32[]{:S(2)}, u32[]{:S(2)}) async-start(bf16[32,4,2048]{2,1,0:T(4,128)(2,1)} %pick.1), calls=%async_computation | async-start | bytes 1048576 | tf_op jit(solution)/shard_map/all_to_all | solution.py:224
  25.5 0.0 copy-done
  25.5 0.1 broadcast_compare_fusion
  25.6 1.0 select_reduce_fusion
  26.5 0.6 fusion.3
  27.2 9.9 %all-to-all-done = bf16[32,4,2048]{2,1,0:T(4,128)(2,1)S(1)} async-done(((bf16[32,4,2048]{2,1,0:T(4,128)(2,1)}), bf16[32,4,2048]{2,1,0:T(4,128)(2,1)S(1)}, u32[]{:S(2)}, u32[]{:S(2)}) %all-to-all-start) | async-done | bytes 524320 | tf_op jit(solution)/shard_map/all_to_all | solution.py:224
  37.0 0.9 reshape.67.refs_3_
  38.0 37.8 %all-gather.3.cloned.1.call-done = bf16[4096,256]{1,0:T(8,128)(2,1)} async-done(((bf16[128,256]{1,0:T(8,128)(2,1)}), bf16[4096,256]{1,0:T(8,128)(2,1)}) %all-gather.3.cloned.1.call-update) | async-done | bytes 2097168 | tf_op jit(solution)/shard_map/all_gather | solution.py:213
  75.7 6.7 %products.1 = (f32[16,128,128]{2,1,0:T(8,128)}, bf16[48,128,128]{2,1,0:T(8,128)(2,1)}) custom-call(s32[64]{0:T(128)} %get-tuple-element.11.refs_0_, s32[64]{0:T(128)} %get-tuple-element.10.refs_1_, bf16[32,128,256]{2,1,0:T(8,128)(2,1)} %bitcast.7, bf16[128,2048]{1,0:T(8,128)(2,1)} %reshape.67.refs_3_), custom_call_target="tpu_custom_call" | custom-call | tf_op jit(solution)/shard_map/products/pallas_call | solution.py:228
  82.4 58.9 %update.1 = (bf16[1,128,128]{2,1,0:T(8,128)(2,1)}, f32[1,128]{1,0:T(1,128)}) custom-call(f32[16,128,128]{2,1,0:T(8,128)} %get-tuple-element.6.kept_part, bf16[48,128,128]{2,1,0:T(8,128)(2,1)} %get-tuple-element.7.cand_part), custom_call_target="tpu_custom_call" | custom-call | tf_op jit(solution)/shard_map/update/pallas_call | solution.py:242
  141.3 1.4 copy.11
  142.7 1.1 copy.12
  (2 shorter events, 0.0 us)
Async XLA Ops:
  7.2 18.3 %copy-start = (s32[32,48]{1,0:T(8,128)S(1)}, s32[32,48]{1,0:T(8,128)}, u32[]{:S(2)}) copy-start(s32[32,48]{1,0:T(8,128)} %param.7) | copy-start | bytes 18436
  7.2 68.5 %all-gather.3.cloned.1.call-start = ((), (), s32[]{:S(2)}) async-start(), calls=%async_computation.1 | async-start | bytes 2162688 | tf_op jit(solution)/shard_map/all_gather | solution.py:213
  15.1 21.9 %all-to-all-start = ((bf16[32,4,2048]{2,1,0:T(4,128)(2,1)}), bf16[32,4,2048]{2,1,0:T(4,128)(2,1)S(1)}, u32[]{:S(2)}, u32[]{:S(2)}) async-start(bf16[32,4,2048]{2,1,0:T(4,128)(2,1)} %pick.1), calls=%async_computation | async-start | bytes 1048576 | tf_op jit(solution)/shard_map/all_to_all | solution.py:224
Sparse Core Ops, SparseCore 0:
  11.1 64.5 all-gather.2

commit v3 on v2

--- a/solution.py
+++ b/solution.py
@@ -97,6 +97,88 @@
     own.start()
     own.wait()
     lax.fori_loop(1, n, finish, 0)
+
+
+def gather_kernel(
+    acts_ref, out_ref, all_ref, in_ref,
+    own_sem, acts_send, acts_recv, relay_send, relay_recv, grad_send, grad_recv,
+):
+    nb = lax.axis_size("blk")
+    b = lax.axis_index("blk")
+    partner = b + 1 - 2 * lax.rem(b, 2)
+    chips = nb // 2
+    barrier = pltpu.get_barrier_semaphore()
+    greet(barrier, "blk", b, nb)
+    pl.semaphore_wait(barrier, nb - 1)
+
+    def remote(src, dst, send, recv, peer):
+        return pltpu.make_async_remote_copy(
+            src_ref=src,
+            dst_ref=dst,
+            send_sem=send,
+            recv_sem=recv,
+            device_id={"blk": peer},
+            device_id_type=MESH,
+        )
+
+    def acts_copy(k, slot):
+        return remote(
+            acts_ref, all_ref.at[slot], acts_send.at[k], acts_recv.at[k], lax.rem(b + 2 * k, nb)
+        )
+
+    def relay_copy(k, slot):
+        return remote(
+            all_ref.at[slot], all_ref.at[slot], relay_send.at[k], relay_recv.at[k], partner
+        )
+
+    def grad_copy(k, slot):
+        peer = lax.rem(b + k, nb)
+        return remote(out_ref.at[peer], in_ref.at[slot], grad_send.at[k], grad_recv.at[k], peer)
+
+    def start_acts(k, carry):
+        acts_copy(k, b).start()
+        return carry
+
+    def start_grad(k, carry):
+        grad_copy(k, b).start()
+        return carry
+
+    own_relay = remote(acts_ref, all_ref.at[b], relay_send.at[0], relay_recv.at[0], partner)
+    lax.fori_loop(1, chips, start_acts, 0)
+    own_relay.start()
+    lax.fori_loop(1, nb, start_grad, 0)
+    own_acts = pltpu.make_async_copy(acts_ref, all_ref.at[b], own_sem.at[0])
+    own_grad = pltpu.make_async_copy(out_ref.at[b], in_ref.at[b], own_sem.at[1])
+    own_acts.start()
+    own_grad.start()
+
+    def relay(k, carry):
+        slot = lax.rem(b + nb - 2 * k, nb)
+        acts_copy(k, slot).wait_recv()
+        relay_copy(k, slot).start()
+        return carry
+
+    lax.fori_loop(1, chips, relay, 0)
+
+    def finish_grad(k, carry):
+        arrived = grad_copy(k, lax.rem(b + nb - k, nb))
+        arrived.wait_send()
+        arrived.wait_recv()
+        return carry
+
+    def finish_acts(k, carry):
+        acts_copy(k, b).wait_send()
+        slot = lax.rem(partner + nb - 2 * k, nb)
+        relay_copy(k, slot).wait_send()
+        relay_copy(k, slot).wait_recv()
+        return carry
+
+    lax.fori_loop(1, nb, finish_grad, 0)
+    own_relay.wait_send()
+    remote(acts_ref, all_ref.at[partner], relay_send.at[0], relay_recv.at[0], partner).wait_recv()
+    lax.fori_loop(1, chips, finish_acts, 0)
+    own_acts.wait()
+    own_grad.wait()
 
 
 def update_kernel(
@@ -210,7 +292,6 @@
     tokens = acts.shape[0]
     per = acts.shape[1] // BLOCK
     slot_ids = jnp.concatenate([kept_ids, cand_ids], axis=1)
-    acts_all = lax.all_gather(acts, "blk", axis=0, tiled=False)
     table, position = column_tables(slot_ids % ncols, width)
     vmem = pl.BlockSpec(memory_space=pltpu.VMEM)
     smem = pl.BlockSpec(memory_space=pltpu.SMEM)
@@ -221,7 +302,28 @@
         out_specs=vmem,
         name="pick",
     )(table.reshape(-1), out_grad)
-    incoming = lax.all_to_all(outgoing, "blk", split_axis=0, concat_axis=0, tiled=True)
+    dma = pltpu.SemaphoreType.DMA
+    chips = owners // 2
+    acts_all, incoming = pl.pallas_call(
+        gather_kernel,
+        out_shape=(
+            jax.ShapeDtypeStruct((owners,) + acts.shape, acts.dtype),
+            jax.ShapeDtypeStruct(outgoing.shape, outgoing.dtype),
+        ),
+        in_specs=[vmem, vmem],
+        out_specs=(vmem, vmem),
+        scratch_shapes=[
+            dma((2,)),
+            dma((chips,)),
+            dma((chips,)),
+            dma((chips,)),
+            dma((chips,)),
+            dma((owners,)),
+            dma((owners,)),
+        ],
+        compiler_params=pltpu.CompilerParams(collective_id=1, has_side_effects=True),
+        name="gather",
+    )(acts, outgoing)
     grad_cols = incoming.reshape(tokens, width * BLOCK)
     my_rows = lax.dynamic_index_in_dim(slot_ids // ncols, owner_index, 0, keepdims=False)
     my_cols = lax.dynamic_index_in_dim(position, owner_index, 0, keepdims=False)
@@ -238,7 +340,6 @@
     toks = lax.axis_size("tok")
     kshare, share = KS // toks, cand_ids.shape[1] // toks
     steps = toks // 2
-    dma = pltpu.SemaphoreType.DMA
     kept_grad, scores = pl.pallas_call(
         update_kernel,
         out_shape=(

time: 151 us -> 118 us (0.78)
  waiting for transfers between devices: 48.3 us -> 0 us
  Pallas kernels: 68.3 us -> 105 us
  between operations: 14.1 us -> 0.69 us
  starting transfers between devices: 10.4 us -> 0 us
    all_gather x1 -> x0, waiting for transfers between devices: 37.8 us -> none  [local(): acts_all = lax.all_gather(acts, 'blk', axis=0, tiled=False)]
    pallas_call x0 -> x1, Pallas kernels: none -> 35 us  [local(): pl.pallas_call(gather_kernel, out_shape=(jax.ShapeDtypeStruct((owners,) +...]
    all_to_all x1 -> x0, starting transfers between devices: 10.4 us -> none  [local(): lax.all_to_all(outgoing, 'blk', split_axis=0, concat_axis=0, tiled=True)]
    all_to_all x1 -> x0, waiting for transfers between devices: 9.87 us -> none  [local(): lax.all_to_all(outgoing, 'blk', split_axis=0, concat_axis=0, tiled=True)]
    pallas_call x1, Pallas kernels: 58.9 us -> 60.8 us  [local(): pl.pallas_call(update_kernel, out_shape=(jax.ShapeDtypeStruct((kshare, BL...]
    unnamed x5 -> x3, local copies, waits for them, and re-layouts: 3.29 us -> 3.28 us
  transfers between devices with their start and end apart: 2 -> 0, of which waited for: 2 -> 0; matrix products, arithmetic and copies ran while one was open for 5% -> 0% of each run, Pallas kernels for 2% -> 0%
where the time goes in v3:
time: 118 us
  Pallas kernels  105 us (89%)
  other arithmetic  6.1 us (5%)
  local copies, waits for them, and re-layouts  5.92 us (5%)
    pallas_call x1, Pallas kernels, local(): pl.pallas_call(update_kernel, out_shape=(jax.ShapeDtypeStruct((kshare, BL...  60.8 us
    pallas_call x1, Pallas kernels, local(): pl.pallas_call(gather_kernel, out_shape=(jax.ShapeDtypeStruct((owners,) +...  35 us
    pallas_call x1, Pallas kernels, local(): pl.pallas_call(lambda *refs: product_kernel(per, *refs), out_shape=(jax.S...  6.67 us
    unnamed x3, local copies, waits for them, and re-layouts  3.28 us
    pallas_call x1, Pallas kernels, local(): pl.pallas_call(lambda *refs: pick_kernel(owners, width, *refs), out_shape...  2.72 us

profile of v3, /device:TPU:1, one launch (start us, length us, event | category | flops | bytes accessed | tf_op | source)
XLA Modules:
  0.0 117.9 jit_solution(14953192642438026461)
XLA Ops:
  0.7 0.8 copy.8
  1.4 0.8 broadcast_compare_fusion
  2.2 0.8 add_select_fusion
  3.0 0.9 fusion
  4.0 0.6 select_reduce_fusion.1
  4.6 0.6 select_reduce_fusion.2
  5.3 1.0 select_reduce_fusion
  6.2 1.3 %fusion.3 = (s32[64]{0:T(128)}, s32[64]{0:T(128)}) fusion(s32[32,64]{1,0:T(8,128)S(1)} %select_reduce_fusion, s32[]{:T(128)S(6)} %select_n.38, pred[32,64]{1,0:T(8,128)(4,1)S(1)} %broadcast_compare_fusion, s32[32,48]{1,0:T(8,128)} %param.7, s32[32,16]{1,0:T(8,128)S(1)} %copy.8), kind=kLoop, calls=%fused_computation.17 | loop fusion | flops 448 | bytes 9028 | tf_op jit(solution)/shard_map/jit(dynamic_index_in_dim)/squeeze | solution.py:329
  7.5 0.7 reshape.66.refs_0_
  8.2 2.7 %pick.1.out_ref = bf16[32,4,2048]{2,1,0:T(4,128)(2,1)} custom-call(s32[512]{0:T(512)} %reshape.66.refs_0_, bf16[4,29568]{1,0:T(4,128)(2,1)} %refs_1_.1), custom_call_target="tpu_custom_call" | custom-call | tf_op jit(solution)/shard_map/pick/pallas_call | solution.py:298
  10.9 35.0 %gather.1 = (bf16[32,128,256]{2,1,0:T(8,128)(2,1)}, bf16[32,4,2048]{2,1,0:T(4,128)(2,1)}) custom-call(bf16[128,256]{1,0:T(8,128)(2,1)} %acts_ref.1, bf16[32,4,2048]{2,1,0:T(4,128)(2,1)} %pick.1.out_ref), custom_call_target="tpu_custom_call" | custom-call | tf_op jit(solution)/shard_map/gather/pallas_call | solution.py:307
  46.0 2.0 %reshape.67.refs_3_ = bf16[128,2048]{1,0:T(8,128)(2,1)} reshape(bf16[32,4,2048]{2,1,0:T(4,128)(2,1)} %get-tuple-element.9) | data formatting | bytes 1048576 | tf_op jit(solution)/shard_map/reshape | solution.py:327
  47.9 6.7 %products.1 = (f32[16,128,128]{2,1,0:T(8,128)}, bf16[48,128,128]{2,1,0:T(8,128)(2,1)}) custom-call(s32[64]{0:T(128)} %get-tuple-element.15.refs_0_, s32[64]{0:T(128)} %get-tuple-element.14.refs_1_, bf16[32,128,256]{2,1,0:T(8,128)(2,1)} %get-tuple-element.8.refs_2_, bf16[128,2048]{1,0:T(8,128)(2,1)} %reshape.67.refs_3_), custom_call_target="tpu_custom_call" | custom-call | tf_op jit(solution)/shard_map/products/pallas_call | solution.py:330
  54.6 60.8 %update.1 = (bf16[1,128,128]{2,1,0:T(8,128)(2,1)}, f32[1,128]{1,0:T(1,128)}) custom-call(f32[16,128,128]{2,1,0:T(8,128)} %get-tuple-element.10.kept_part, bf16[48,128,128]{2,1,0:T(8,128)(2,1)} %get-tuple-element.11.cand_part), custom_call_target="tpu_custom_call" | custom-call | tf_op jit(solution)/shard_map/update/pallas_call | solution.py:343
  115.4 1.4 %copy.11 = bf16[1,1,128,128]{3,2,1,0:T(8,128)(2,1)} copy(bf16[1,1,128,128]{3,2,1,0:T(8,128)(2,1)} %bitcast.6) | data formatting | bytes 65536
  116.7 1.1 copy.12
  (2 shorter events, 0.0 us)

commit v4 on v3

--- a/solution.py
+++ b/solution.py
@@ -1,3 +1,5 @@
+import math
+
 import jax
 import jax.numpy as jnp
 from jax import lax
@@ -34,30 +36,6 @@
     lax.fori_loop(0, owners, one_owner, 0)
 
 
-def product_kernel(per, rows_ref, cols_ref, acts_ref, grad_ref, kept_ref, cand_ref):
-    def product(slot):
-        row = rows_ref[slot]
-        col = cols_ref[slot]
-        left = acts_ref[row // per, :, pl.ds(pl.multiple_of((row % per) * BLOCK, BLOCK), BLOCK)]
-        right = grad_ref[:, pl.ds(pl.multiple_of(col * BLOCK, BLOCK), BLOCK)]
-        return lax.dot_general(
-            left, right, (((0,), (0,)), ((), ())), preferred_element_type=jnp.float32
-        )
-
-    def kept(j, carry):
-        for u in range(4):
-            kept_ref[4 * j + u] = product(4 * j + u)
-        return carry
-
-    def cand(j, carry):
-        for u in range(4):
-            cand_ref[4 * j + u] = product(kept_ref.shape[0] + 4 * j + u).astype(cand_ref.dtype)
-        return carry
-
-    lax.fori_loop(0, kept_ref.shape[0] // 4, kept, 0)
-    lax.fori_loop(0, cand_ref.shape[0] // 4, cand, 0)
-
-
 MESH = pl.DeviceIdType.MESH
 
 
@@ -106,7 +84,7 @@
     nb = lax.axis_size("blk")
     b = lax.axis_index("blk")
     partner = b + 1 - 2 * lax.rem(b, 2)
-    chips = nb // 2
+    side = acts_send.shape[1]
     barrier = pltpu.get_barrier_semaphore()
     greet(barrier, "blk", b, nb)
     pl.semaphore_wait(barrier, nb - 1)
@@ -121,44 +99,85 @@
             device_id_type=MESH,
         )
 
-    def acts_copy(k, slot):
+    core = lax.rem(b, 2)
+    spot = (lax.rem(b // 2, side), b // (2 * side))
+    halves = tuple(
+        acts_ref.at[:, pl.ds(h * BLOCK, BLOCK)] for h in range(2)
+    )
+
+    def device(h, first, second):
+        p = lax.rem(spot[h] + first + side, side)
+        q = lax.rem(spot[1 - h] + second + side, side)
+        x, y = (p, q) if h == 0 else (q, p)
+        return (y * side + x) * 2 + core
+
+    def held(h, i, j):
+        return all_ref.at[device(h, -i, -j), h]
+
+    def hop(h, i, j, step):
+        i0, j0 = (i - step[0]) % side, (j - step[1]) % side
+        here = halves[h] if i0 == 0 and j0 == 0 else held(h, i0, j0)
         return remote(
-            acts_ref, all_ref.at[slot], acts_send.at[k], acts_recv.at[k], lax.rem(b + 2 * k, nb)
-        )
-
-    def relay_copy(k, slot):
-        return remote(
-            all_ref.at[slot], all_ref.at[slot], relay_send.at[k], relay_recv.at[k], partner
-        )
+            here,
+            held(h, i0, j0),
+            acts_send.at[h, i, j],
+            acts_recv.at[h, i, j],
+            device(h, step[0], step[1]),
+        )
+
+    def landing(h, i, j):
+        return remote(held(h, i, j), held(h, i, j), acts_send.at[h, i, j], acts_recv.at[h, i, j], partner)
+
+    def relay_copy(h, i, j):
+        here = halves[h] if i == 0 and j == 0 else held(h, i, j)
+        return remote(here, held(h, i, j), relay_send.at[h, i, j], relay_recv.at[h, i, j], partner)
+
+    def relay_landing(h, i, j):
+        block = all_ref.at[device(h, -i, -j) + 1 - 2 * core, h]
+        return remote(block, block, relay_send.at[h, i, j], relay_recv.at[h, i, j], partner)
+
+    def forward(h, i, j):
+        way = 1 if h == 0 else -1
+        if j == 0:
+            if i == 0:
+                hop(h, 1, 0, (1, 0)).start()
+                hop(h, side - 1, 0, (-1, 0)).start()
+            elif i == way % side:
+                hop(h, 2, 0, (way, 0)).start()
+            hop(h, i, 1, (0, 1)).start()
+            hop(h, i, side - 1, (0, -1)).start()
+        elif j == way % side:
+            hop(h, i, 2, (0, way)).start()
+        relay_copy(h, i, j).start()
+
+    def arrive(h, i, j):
+        landing(h, i, j).wait_recv()
+        forward(h, i, j)
 
     def grad_copy(k, slot):
         peer = lax.rem(b + k, nb)
         return remote(out_ref.at[peer], in_ref.at[slot], grad_send.at[k], grad_recv.at[k], peer)
 
-    def start_acts(k, carry):
-        acts_copy(k, b).start()
-        return carry
-
     def start_grad(k, carry):
         grad_copy(k, b).start()
         return carry
 
-    own_relay = remote(acts_ref, all_ref.at[b], relay_send.at[0], relay_recv.at[0], partner)
-    lax.fori_loop(1, chips, start_acts, 0)
-    own_relay.start()
+    for h in range(2):
+        forward(h, 0, 0)
+    for i, j in ((1, 0), (3, 0), (0, 1), (0, 3)):
+        for h in range(2):
+            arrive(h, i, j)
     lax.fori_loop(1, nb, start_grad, 0)
-    own_acts = pltpu.make_async_copy(acts_ref, all_ref.at[b], own_sem.at[0])
-    own_grad = pltpu.make_async_copy(out_ref.at[b], in_ref.at[b], own_sem.at[1])
-    own_acts.start()
-    own_grad.start()
-
-    def relay(k, carry):
-        slot = lax.rem(b + nb - 2 * k, nb)
-        acts_copy(k, slot).wait_recv()
-        relay_copy(k, slot).start()
-        return carry
-
-    lax.fori_loop(1, chips, relay, 0)
+    own_acts = [
+        pltpu.make_async_copy(halves[h], all_ref.at[b, h], own_sem.at[h]) for h in range(2)
+    ]
+    own_grad = pltpu.make_async_copy(out_ref.at[b], in_ref.at[b], own_sem.at[2])
+    for own in (*own_acts, own_grad):
+        own.start()
+    later = ((2, 0), (0, 2), (1, 1), (1, 3), (3, 1), (3, 3), (1, 2), (3, 2), (2, 1), (2, 3), (2, 2))
+    for i, j in later:
+        for h in range(2):
+            arrive(h, i, j)
 
     def finish_grad(k, carry):
         arrived = grad_copy(k, lax.rem(b + nb - k, nb))
@@ -166,24 +185,21 @@
         arrived.wait_recv()
         return carry
 
-    def finish_acts(k, carry):
-        acts_copy(k, b).wait_send()
-        slot = lax.rem(partner + nb - 2 * k, nb)
-        relay_copy(k, slot).wait_send()
-        relay_copy(k, slot).wait_recv()
-        return carry
-
     lax.fori_loop(1, nb, finish_grad, 0)
-    own_relay.wait_send()
-    remote(acts_ref, all_ref.at[partner], relay_send.at[0], relay_recv.at[0], partner).wait_recv()
-    lax.fori_loop(1, chips, finish_acts, 0)
-    own_acts.wait()
-    own_grad.wait()
+    for h in range(2):
+        for i in range(side):
+            for j in range(side):
+                if i or j:
+                    landing(h, i, j).wait_send()
+                relay_landing(h, i, j).wait_send()
+                relay_landing(h, i, j).wait_recv()
+    for own in (*own_acts, own_grad):
+        own.wait()
 
 
 def update_kernel(
-    kept_part, cand_part, kept_ref, score_ref,
-    kept_buf, cand_buf, send_sems, recv_sems,
+    row_ref, col_ref, acts_ref, grad_ref, kept_ref, score_ref,
+    cols, kept_buf, cand_buf, send_sems, recv_sems,
     norm_buf, mine, line, plane, own_sem, line_send, line_recv, plane_send, plane_recv,
 ):
     nt, nb = lax.axis_size("tok"), lax.axis_size("blk")
@@ -199,10 +215,16 @@
     greet(barrier, "tok", t, nt)
     greet(barrier, "blk", b, nb)
 
+    for w in range(cols.shape[0]):
+        cols[w] = grad_ref[:, w * BLOCK : (w + 1) * BLOCK]
+
     def product(d, j):
-        if j < kshare:
-            return kept_part[d * kshare + j]
-        return cand_part[d * cshare + (j - kshare)].astype(jnp.float32)
+        slot = d * kshare + j if j < kshare else nt * kshare + d * cshare + (j - kshare)
+        left = acts_ref[row_ref[slot]]
+        right = cols[col_ref[slot]]
+        return lax.dot_general(
+            left, right, (((0,), (0,)), ((), ())), preferred_element_type=jnp.float32
+        )
 
     def home(way, step):
         if way == 0:
@@ -303,40 +325,31 @@
         name="pick",
     )(table.reshape(-1), out_grad)
     dma = pltpu.SemaphoreType.DMA
-    chips = owners // 2
+    side = math.isqrt(owners // 2)
     acts_all, incoming = pl.pallas_call(
         gather_kernel,
         out_shape=(
-            jax.ShapeDtypeStruct((owners,) + acts.shape, acts.dtype),
+            jax.ShapeDtypeStruct((owners, per, tokens, BLOCK), acts.dtype),
             jax.ShapeDtypeStruct(outgoing.shape, outgoing.dtype),
         ),
         in_specs=[vmem, vmem],
         out_specs=(vmem, vmem),
         scratch_shapes=[
-            dma((2,)),
-            dma((chips,)),
-            dma((chips,)),
-            dma((chips,)),
-            dma((chips,)),
+            dma((3,)),
+            dma((per, side, side)),
+            dma((per, side, side)),
+            dma((per, side, side)),
+            dma((per, side, side)),
             dma((owners,)),
             dma((owners,)),
         ],
         compiler_params=pltpu.CompilerParams(collective_id=1, has_side_effects=True),
         name="gather",
     )(acts, outgoing)
+    acts_all = acts_all.reshape(owners * per, tokens, BLOCK)
     grad_cols = incoming.reshape(tokens, width * BLOCK)
     my_rows = lax.dynamic_index_in_dim(slot_ids // ncols, owner_index, 0, keepdims=False)
     my_cols = lax.dynamic_index_in_dim(position, owner_index, 0, keepdims=False)
-    kept_part, cand_part = pl.pallas_call(
-        lambda *refs: product_kernel(per, *refs),
-        out_shape=(
-            jax.ShapeDtypeStruct((KS, BLOCK, BLOCK), jnp.float32),
-            jax.ShapeDtypeStruct((cand_ids.shape[1], BLOCK, BLOCK), jnp.bfloat16),
-        ),
-        in_specs=[smem, smem, vmem, vmem],
-        out_specs=(vmem, vmem),
-        name="products",
-    )(my_rows, my_cols, acts_all, grad_cols)
     toks = lax.axis_size("tok")
     kshare, share = KS // toks, cand_ids.shape[1] // toks
     steps = toks // 2
@@ -346,9 +359,10 @@
             jax.ShapeDtypeStruct((kshare, BLOCK, BLOCK), jnp.bfloat16),
             jax.ShapeDtypeStruct((1, BLOCK), jnp.float32),
         ),
-        in_specs=[vmem, vmem],
+        in_specs=[smem, smem, vmem, vmem],
         out_specs=(vmem, vmem),
         scratch_shapes=[
+            pltpu.VMEM((width, tokens, BLOCK), grad_cols.dtype),
             pltpu.VMEM((2, steps + 1, kshare, BLOCK, BLOCK), jnp.float32),
             pltpu.VMEM((2, steps + 1, share, BLOCK, BLOCK), jnp.bfloat16),
             dma((2, steps, kshare + share)),
@@ -365,7 +379,7 @@
         ],
         compiler_params=pltpu.CompilerParams(collective_id=0, has_side_effects=True),
         name="update",
-    )(kept_part, cand_part)
+    )(my_rows, my_cols, acts_all, grad_cols)
     cand_score = scores[:, :share]
     return (kept_grad[None], cand_score)
 

time: 118 us -> 112 us (0.949)
  Pallas kernels: 105 us -> 99 us
    pallas_call x2 -> x1, Pallas kernels: 41.7 us -> 33.4 us  [local(): pl.pallas_call(gather_kernel, out_shape=(jax.ShapeDtypeStruct((owners, pe...]
    pallas_call x1, Pallas kernels: 60.8 us -> 62.9 us  [local(): pl.pallas_call(update_kernel, out_shape=(jax.ShapeDtypeStruct((kshare, BL...]
where the time goes in v4:
time: 112 us
  Pallas kernels  99 us (88%)
  other arithmetic  6.04 us (5%)
  local copies, waits for them, and re-layouts  5.87 us (5%)
    pallas_call x1, Pallas kernels, local(): pl.pallas_call(update_kernel, out_shape=(jax.ShapeDtypeStruct((kshare, BL...  62.9 us
    pallas_call x1, Pallas kernels, local(): pl.pallas_call(gather_kernel, out_shape=(jax.ShapeDtypeStruct((owners, pe...  33.4 us
    unnamed x3, local copies, waits for them, and re-layouts  3.26 us
    pallas_call x1, Pallas kernels, local(): pl.pallas_call(lambda *refs: pick_kernel(owners, width, *refs), out_shape...  2.71 us

profile of v4, /device:TPU:1, one launch (start us, length us, event | category | flops | bytes accessed | tf_op | source)
XLA Modules:
  0.0 111.6 jit_solution(9421076342331111369)
XLA Ops:
  0.7 0.8 copy.8
  1.4 0.8 broadcast_compare_fusion
  2.2 0.8 add_select_fusion
  3.0 0.9 fusion
  4.0 0.6 select_reduce_fusion.1
  4.6 0.6 select_reduce_fusion.2
  5.3 1.0 select_reduce_fusion
  6.2 1.3 %fusion.3 = (s32[64]{0:T(128)}, s32[64]{0:T(128)}) fusion(s32[32,64]{1,0:T(8,128)S(1)} %select_reduce_fusion, s32[]{:T(128)S(6)} %select_n.38, pred[32,64]{1,0:T(8,128)(4,1)S(1)} %broadcast_compare_fusion, s32[32,48]{1,0:T(8,128)} %param.7, s32[32,16]{1,0:T(8,128)S(1)} %copy.8), kind=kLoop, calls=%fused_computation.17 | loop fusion | flops 448 | bytes 9028 | tf_op jit(solution)/shard_map/jit(dynamic_index_in_dim)/squeeze | solution.py:352
  7.5 0.7 reshape.69.refs_0_
  8.1 2.7 %pick.1.out_ref = bf16[32,4,2048]{2,1,0:T(4,128)(2,1)} custom-call(s32[512]{0:T(512)} %reshape.69.refs_0_, bf16[4,29568]{1,0:T(4,128)(2,1)} %refs_1_.1), custom_call_target="tpu_custom_call" | custom-call | tf_op jit(solution)/shard_map/pick/pallas_call | solution.py:320
  10.8 33.4 %gather.1 = (bf16[32,2,128,128]{3,2,1,0:T(8,128)(2,1)}, bf16[32,4,2048]{2,1,0:T(4,128)(2,1)}) custom-call(bf16[128,256]{1,0:T(8,128)(2,1)} %acts_ref.1, bf16[32,4,2048]{2,1,0:T(4,128)(2,1)} %pick.1.out_ref), custom_call_target="tpu_custom_call" | custom-call | tf_op jit(solution)/shard_map/gather/pallas_call | solution.py:329
  44.3 2.0 %reshape.71.grad_ref = bf16[128,2048]{1,0:T(8,128)(2,1)} reshape(bf16[32,4,2048]{2,1,0:T(4,128)(2,1)} %get-tuple-element.7) | data formatting | bytes 1048576 | tf_op jit(solution)/shard_map/reshape | solution.py:350
  46.2 62.9 %update.1 = (bf16[1,128,128]{2,1,0:T(8,128)(2,1)}, f32[1,128]{1,0:T(1,128)}) custom-call(s32[64]{0:T(128)} %get-tuple-element.11.row_ref, s32[64]{0:T(128)} %get-tuple-element.10.col_ref, bf16[64,128,128]{2,1,0:T(8,128)(2,1)} %bitcast.7, bf16[128,2048]{1,0:T(8,128)(2,1)} %reshape.71.grad_ref), custom_call_target="tpu_custom_call" | custom-call | tf_op jit(solution)/shard_map/update/pallas_call | solution.py:356
  109.2 1.4 %copy.11 = bf16[1,1,128,128]{3,2,1,0:T(8,128)(2,1)} copy(bf16[1,1,128,128]{3,2,1,0:T(8,128)(2,1)} %bitcast.8) | data formatting | bytes 65536
  110.5 1.1 copy.12
  (2 shorter events, 0.0 us)

commit v5 on v4

--- a/solution.py
+++ b/solution.py
@@ -77,7 +77,7 @@
     lax.fori_loop(1, n, finish, 0)
 
 
-def gather_kernel(
+def gather(
     acts_ref, out_ref, all_ref, in_ref,
     own_sem, acts_send, acts_recv, relay_send, relay_recv, grad_send, grad_recv,
 ):
@@ -85,9 +85,7 @@
     b = lax.axis_index("blk")
     partner = b + 1 - 2 * lax.rem(b, 2)
     side = acts_send.shape[1]
-    barrier = pltpu.get_barrier_semaphore()
-    greet(barrier, "blk", b, nb)
-    pl.semaphore_wait(barrier, nb - 1)
+    per = acts_send.shape[0]
 
     def remote(src, dst, send, recv, peer):
         return pltpu.make_async_remote_copy(
@@ -112,7 +110,7 @@
         return (y * side + x) * 2 + core
 
     def held(h, i, j):
-        return all_ref.at[device(h, -i, -j), h]
+        return all_ref.at[device(h, -i, -j) * per + h]
 
     def hop(h, i, j, step):
         i0, j0 = (i - step[0]) % side, (j - step[1]) % side
@@ -133,7 +131,7 @@
         return remote(here, held(h, i, j), relay_send.at[h, i, j], relay_recv.at[h, i, j], partner)
 
     def relay_landing(h, i, j):
-        block = all_ref.at[device(h, -i, -j) + 1 - 2 * core, h]
+        block = all_ref.at[(device(h, -i, -j) + 1 - 2 * core) * per + h]
         return remote(block, block, relay_send.at[h, i, j], relay_recv.at[h, i, j], partner)
 
     def forward(h, i, j):
@@ -169,7 +167,7 @@
             arrive(h, i, j)
     lax.fori_loop(1, nb, start_grad, 0)
     own_acts = [
-        pltpu.make_async_copy(halves[h], all_ref.at[b, h], own_sem.at[h]) for h in range(2)
+        pltpu.make_async_copy(halves[h], all_ref.at[b * per + h], own_sem.at[h]) for h in range(2)
     ]
     own_grad = pltpu.make_async_copy(out_ref.at[b], in_ref.at[b], own_sem.at[2])
     for own in (*own_acts, own_grad):
@@ -198,7 +196,8 @@
 
 
 def update_kernel(
-    row_ref, col_ref, acts_ref, grad_ref, kept_ref, score_ref,
+    row_ref, col_ref, acts_ref, out_ref, kept_ref, score_ref,
+    all_ref, in_ref, gather_own, acts_send, acts_recv, relay_send, relay_recv, grad_send, grad_recv,
     cols, kept_buf, cand_buf, send_sems, recv_sems,
     norm_buf, mine, line, plane, own_sem, line_send, line_recv, plane_send, plane_recv,
 ):
@@ -214,13 +213,18 @@
     barrier = pltpu.get_barrier_semaphore()
     greet(barrier, "tok", t, nt)
     greet(barrier, "blk", b, nb)
-
+    pl.semaphore_wait(barrier, nt + nb - 2)
+    gather(
+        acts_ref, out_ref, all_ref, in_ref,
+        gather_own, acts_send, acts_recv, relay_send, relay_recv, grad_send, grad_recv,
+    )
     for w in range(cols.shape[0]):
-        cols[w] = grad_ref[:, w * BLOCK : (w + 1) * BLOCK]
+        rows = in_ref[:, :, w * BLOCK : (w + 1) * BLOCK].astype(jnp.float32)
+        cols[w] = rows.reshape(cols.shape[1:]).astype(cols.dtype)
 
     def product(d, j):
         slot = d * kshare + j if j < kshare else nt * kshare + d * cshare + (j - kshare)
-        left = acts_ref[row_ref[slot]]
+        left = all_ref[row_ref[slot]]
         right = cols[col_ref[slot]]
         return lax.dot_general(
             left, right, (((0,), (0,)), ((), ())), preferred_element_type=jnp.float32
@@ -257,7 +261,6 @@
         for j in range(blocks):
             here = block(way, 0, j)
             here[...] = product(home(way, 0), j).astype(here.dtype)
-    pl.semaphore_wait(barrier, nt + nb - 2)
     for j in range(blocks):
         for way in range(2):
             copy(way, 0, j).start()
@@ -326,28 +329,6 @@
     )(table.reshape(-1), out_grad)
     dma = pltpu.SemaphoreType.DMA
     side = math.isqrt(owners // 2)
-    acts_all, incoming = pl.pallas_call(
-        gather_kernel,
-        out_shape=(
-            jax.ShapeDtypeStruct((owners, per, tokens, BLOCK), acts.dtype),
-            jax.ShapeDtypeStruct(outgoing.shape, outgoing.dtype),
-        ),
-        in_specs=[vmem, vmem],
-        out_specs=(vmem, vmem),
-        scratch_shapes=[
-            dma((3,)),
-            dma((per, side, side)),
-            dma((per, side, side)),
-            dma((per, side, side)),
-            dma((per, side, side)),
-            dma((owners,)),
-            dma((owners,)),
-        ],
-        compiler_params=pltpu.CompilerParams(collective_id=1, has_side_effects=True),
-        name="gather",
-    )(acts, outgoing)
-    acts_all = acts_all.reshape(owners * per, tokens, BLOCK)
-    grad_cols = incoming.reshape(tokens, width * BLOCK)
     my_rows = lax.dynamic_index_in_dim(slot_ids // ncols, owner_index, 0, keepdims=False)
     my_cols = lax.dynamic_index_in_dim(position, owner_index, 0, keepdims=False)
     toks = lax.axis_size("tok")
@@ -362,7 +343,16 @@
         in_specs=[smem, smem, vmem, vmem],
         out_specs=(vmem, vmem),
         scratch_shapes=[
-            pltpu.VMEM((width, tokens, BLOCK), grad_cols.dtype),
+            pltpu.VMEM((owners * per, tokens, BLOCK), acts.dtype),
+            pltpu.VMEM(outgoing.shape, outgoing.dtype),
+            dma((3,)),
+            dma((per, side, side)),
+            dma((per, side, side)),
+            dma((per, side, side)),
+            dma((per, side, side)),
+            dma((owners,)),
+            dma((owners,)),
+            pltpu.VMEM((width, tokens, BLOCK), outgoing.dtype),
             pltpu.VMEM((2, steps + 1, kshare, BLOCK, BLOCK), jnp.float32),
             pltpu.VMEM((2, steps + 1, share, BLOCK, BLOCK), jnp.bfloat16),
             dma((2, steps, kshare + share)),
@@ -379,7 +369,7 @@
         ],
         compiler_params=pltpu.CompilerParams(collective_id=0, has_side_effects=True),
         name="update",
-    )(my_rows, my_cols, acts_all, grad_cols)
+    )(my_rows, my_cols, acts, outgoing)
     cand_score = scores[:, :share]
     return (kept_grad[None], cand_score)
 

time: 112 us -> 101 us (0.902)
  Pallas kernels: 99 us -> 92.3 us
  local copies, waits for them, and re-layouts: 5.87 us -> 3.29 us
  other arithmetic: 6.04 us -> 4.02 us
    pallas_call x1 -> x0, Pallas kernels: 33.4 us -> none  [local(): pl.pallas_call(gather_kernel, out_shape=(jax.ShapeDtypeStruct((owners, pe...]
    pallas_call x1, Pallas kernels: 62.9 us -> 89.6 us  [local(): pl.pallas_call(update_kernel, out_shape=(jax.ShapeDtypeStruct((kshare, BL...]
    reshape x1 -> x0, local copies, waits for them, and re-layouts: 1.96 us -> none  [local(): grad_cols = incoming.reshape(tokens, width * BLOCK)]
    unnamed x3 -> x9, local copies, waits for them, and re-layouts: 3.26 us -> 2.63 us
where the time goes in v5:
time: 101 us; the launch traced here: 100 us
  Pallas kernels  92.3 us (91%)
  other arithmetic  4.02 us (4%)
  local copies, waits for them, and re-layouts  3.29 us (3%)
    pallas_call x1, Pallas kernels, local(): pl.pallas_call(update_kernel, out_shape=(jax.ShapeDtypeStruct((kshare, BL...  89.6 us
    pallas_call x1, Pallas kernels, local(): pl.pallas_call(lambda *refs: pick_kernel(owners, width, *refs), out_shape...  2.7 us
    unnamed x9, local copies, waits for them, and re-layouts  2.63 us

profile of v5, /device:TPU:1, one launch (start us, length us, event | category | flops | bytes accessed | tf_op | source)
XLA Modules:
  0.0 100.3 jit_solution(6539426686013643950)
XLA Ops:
  0.6 0.0 copy-start.1
  0.6 0.0 copy-start
  0.7 0.7 copy-done.1
  1.3 0.1 copy.8
  1.4 0.0 copy-done
  1.4 0.1 broadcast_compare_fusion
  1.5 0.1 add_select_fusion
  1.6 0.9 fusion
  2.6 0.6 select_reduce_fusion.1
  3.2 0.6 select_reduce_fusion.2
  3.8 1.0 select_reduce_fusion
  4.8 0.7 fusion.3
  5.4 0.7 reshape.63.refs_0_
  6.1 2.7 %pick.1.out_ref = bf16[32,4,2048]{2,1,0:T(4,128)(2,1)} custom-call(s32[512]{0:T(512)} %reshape.63.refs_0_, bf16[4,29568]{1,0:T(4,128)(2,1)} %refs_1_.1), custom_call_target="tpu_custom_call" | custom-call | tf_op jit(solution)/shard_map/pick/pallas_call | solution.py:323
  8.8 89.6 %update.1 = (bf16[1,128,128]{2,1,0:T(8,128)(2,1)}, f32[1,128]{1,0:T(1,128)}) custom-call(s32[64]{0:T(128)} %get-tuple-element.7.row_ref, s32[64]{0:T(128)} %get-tuple-element.6.col_ref, bf16[128,256]{1,0:T(8,128)(2,1)} %acts_ref.1, bf16[32,4,2048]{2,1,0:T(4,128)(2,1)} %pick.1.out_ref), custom_call_target="tpu_custom_call" | custom-call | tf_op jit(solution)/shard_map/update/pallas_call | solution.py:337
  98.4 0.0 copy-start.2
  98.5 1.4 %copy.11 = bf16[1,1,128,128]{3,2,1,0:T(8,128)(2,1)} copy(bf16[1,1,128,128]{3,2,1,0:T(8,128)(2,1)} %bitcast.6) | data formatting | bytes 65536
  99.8 0.0 copy-done.2
  99.8 0.5 copy.12
  (2 shorter events, 0.0 us)
Async XLA Ops:
  0.6 0.7 copy-start.1
  0.6 0.8 copy-start
  98.4 1.4 %copy-start.2 = (f32[1,128]{1,0:T(1,128)S(1)}, f32[1,128]{1,0:T(1,128)}, u32[]{:S(2)}) copy-start(f32[1,128]{1,0:T(1,128)} %get-tuple-element.5) | copy-start | bytes 1540

commit v6 on v5

--- a/solution.py
+++ b/solution.py
@@ -60,21 +60,25 @@
             device_id_type=MESH,
         )
 
-    def start(k, carry):
+    def start_one(k, carry):
         copy(k, me).start()
         return carry
 
-    def finish(k, carry):
+    def finish_one(k, carry):
         arrived = copy(k, lax.rem(me + n - k, n))
         arrived.wait_send()
         arrived.wait_recv()
         return carry
 
-    lax.fori_loop(1, n, start, 0)
-    own = pltpu.make_async_copy(src, buf.at[me], own_sem)
-    own.start()
-    own.wait()
-    lax.fori_loop(1, n, finish, 0)
+    def start():
+        lax.fori_loop(1, n, start_one, 0)
+        pltpu.make_async_copy(src, buf.at[me], own_sem).start()
+
+    def finish():
+        pltpu.make_async_copy(src, buf.at[me], own_sem).wait()
+        lax.fori_loop(1, n, finish_one, 0)
+
+    return start, finish
 
 
 def gather(
@@ -257,40 +261,72 @@
         here[...] = (here[...].astype(jnp.float32) + term).astype(here.dtype)
         copy(way, step, j).start()
 
-    for way in range(2):
-        for j in range(blocks):
-            here = block(way, 0, j)
-            here[...] = product(home(way, 0), j).astype(here.dtype)
-    for j in range(blocks):
-        for way in range(2):
-            copy(way, 0, j).start()
-
-    def both(step, carry):
-        for j in range(blocks):
+    kept, cand = range(kshare), range(kshare, blocks)
+
+    def begin(js):
+        for j in js:
+            for way in range(2):
+                here = block(way, 0, j)
+                here[...] = product(home(way, 0), j).astype(here.dtype)
+        for j in js:
+            for way in range(2):
+                copy(way, 0, j).start()
+
+    def both(step, js):
+        for j in js:
             for way in range(2):
                 advance(way, step, j)
-        return carry
-
-    lax.fori_loop(1, down_hops, both, 0)
+
+    def total(j):
+        value = product(t, j)
+        for way in (1, 0):
+            copy(way, hops[way] - 1, j).wait_recv()
+            value = value + block(way, hops[way], j)[...].astype(jnp.float32)
+        return value
+
+    lag = down_hops // 2
+
+    def cand_only(step, carry):
+        both(step, cand)
+        return carry
+
+    def cand_and_kept(step, carry):
+        both(step, cand)
+        both(step - lag, kept)
+        return carry
+
+    begin(cand)
+    lax.fori_loop(1, lag + 1, cand_only, 0)
+    begin(kept)
+    lax.fori_loop(lag + 1, down_hops, cand_and_kept, 0)
     for step in range(down_hops, up_hops):
-        for j in range(blocks):
+        for j in cand:
             advance(0, step, j)
+        both(step - lag, kept)
 
     lane = lax.broadcasted_iota(jnp.int32, norm_buf.shape, 1)
     squares = jnp.zeros(norm_buf.shape, jnp.float32)
-    for j in range(blocks):
-        total = product(t, j)
-        for way in (1, 0):
-            copy(way, hops[way] - 1, j).wait_recv()
-            total = total + block(way, hops[way], j)[...].astype(jnp.float32)
-        if j < kshare:
-            kept_ref[j] = total.astype(kept_ref.dtype)
-        else:
-            squares = jnp.where(lane == j - kshare, jnp.sum(total * total), squares)
+    for j in cand:
+        value = total(j)
+        squares = jnp.where(lane == j - kshare, jnp.sum(value * value), squares)
     norms = jnp.sqrt(squares)
     norm_buf[...] = norms
     own = pltpu.make_async_copy(norm_buf, mine, own_sem)
     own.start()
+    own.wait()
+
+    start, finish = exchange("tok", t, nt, mine, line, line_send, line_recv, own_sem)
+    start()
+    for step in range(up_hops - lag, down_hops):
+        both(step, kept)
+    finish()
+    start, finish = exchange("blk", b, nb, line, plane, plane_send, plane_recv, own_sem)
+    start()
+    for step in range(down_hops, up_hops):
+        for j in kept:
+            advance(0, step, j)
+    for j in kept:
+        kept_ref[j] = total(j).astype(kept_ref.dtype)
 
     def sent(step, carry):
         for way in range(2):
@@ -302,10 +338,7 @@
     for step in range(down_hops, up_hops):
         for j in range(blocks):
             copy(0, step, j).wait_send()
-    own.wait()
-
-    exchange("tok", t, nt, mine, line, line_send, line_recv, own_sem)
-    exchange("blk", b, nb, line, plane, plane_send, plane_recv, own_sem)
+    finish()
     score_ref[...] = norms / (jnp.max(plane[...]) + 1e-06)
 
 

time: 101 us -> 97.9 us (0.969)
  Pallas kernels: 92.3 us -> 89.6 us
    pallas_call x1, Pallas kernels: 89.6 us -> 86.9 us  [local(): pl.pallas_call(update_kernel, out_shape=(jax.ShapeDtypeStruct((kshare, BL...]
where the time goes in v6:
time: 97.9 us; the launch traced here: 97.6 us
  Pallas kernels  89.6 us (92%)
  other arithmetic  4.02 us (4%)
  local copies, waits for them, and re-layouts  3.29 us (3%)
    pallas_call x1, Pallas kernels, local(): pl.pallas_call(update_kernel, out_shape=(jax.ShapeDtypeStruct((kshare, BL...  86.9 us
    pallas_call x1, Pallas kernels, local(): pl.pallas_call(lambda *refs: pick_kernel(owners, width, *refs), out_shape...  2.7 us
    unnamed x9, local copies, waits for them, and re-layouts  2.63 us

profile of v6, /device:TPU:1, one launch (start us, length us, event | category | flops | bytes accessed | tf_op | source)
XLA Modules:
  0.0 97.6 jit_solution(874718657982286986)
XLA Ops:
  0.6 0.0 copy-start.1
  0.6 0.0 copy-start
  0.7 0.7 copy-done.1
  1.3 0.1 copy.8
  1.4 0.0 copy-done
  1.4 0.1 broadcast_compare_fusion
  1.5 0.1 add_select_fusion
  1.6 0.9 fusion
  2.6 0.6 select_reduce_fusion.1
  3.2 0.6 select_reduce_fusion.2
  3.8 1.0 select_reduce_fusion
  4.8 0.7 fusion.3
  5.4 0.7 reshape.63.refs_0_
  6.1 2.7 %pick.1.out_ref = bf16[32,4,2048]{2,1,0:T(4,128)(2,1)} custom-call(s32[512]{0:T(512)} %reshape.63.refs_0_, bf16[4,29568]{1,0:T(4,128)(2,1)} %refs_1_.1), custom_call_target="tpu_custom_call" | custom-call | tf_op jit(solution)/shard_map/pick/pallas_call | solution.py:356
  8.8 86.9 %update.1 = (bf16[1,128,128]{2,1,0:T(8,128)(2,1)}, f32[1,128]{1,0:T(1,128)}) custom-call(s32[64]{0:T(128)} %get-tuple-element.7.row_ref, s32[64]{0:T(128)} %get-tuple-element.6.col_ref, bf16[128,256]{1,0:T(8,128)(2,1)} %acts_ref.1, bf16[32,4,2048]{2,1,0:T(4,128)(2,1)} %pick.1.out_ref), custom_call_target="tpu_custom_call" | custom-call | tf_op jit(solution)/shard_map/update/pallas_call | solution.py:370
  95.7 0.0 copy-start.2
  95.8 1.4 %copy.11 = bf16[1,1,128,128]{3,2,1,0:T(8,128)(2,1)} copy(bf16[1,1,128,128]{3,2,1,0:T(8,128)(2,1)} %bitcast.6) | data formatting | bytes 65536
  97.1 0.0 copy-done.2
  97.1 0.5 copy.12
  (2 shorter events, 0.0 us)
Async XLA Ops:
  0.6 0.7 copy-start.1
  0.6 0.8 copy-start
  95.7 1.4 %copy-start.2 = (f32[1,128]{1,0:T(1,128)S(1)}, f32[1,128]{1,0:T(1,128)}, u32[]{:S(2)}) copy-start(f32[1,128]{1,0:T(1,128)} %get-tuple-element.5) | copy-start | bytes 1540

commit v7 on v6

--- a/solution.py
+++ b/solution.py
@@ -244,22 +244,33 @@
             return kept_buf.at[way, step, j]
         return cand_buf.at[way, step, j - kshare]
 
-    def copy(way, step, j):
+    def parts(j):
+        return range(2 if j < kshare else 1)
+
+    def piece(way, step, j, part):
+        if j < kshare:
+            return block(way, step, j).at[pl.ds(part * (BLOCK // 2), BLOCK // 2)]
+        return block(way, step, j)
+
+    def copy(way, step, j, part):
         return pltpu.make_async_remote_copy(
-            src_ref=block(way, step, j),
-            dst_ref=block(way, step + 1, j),
-            send_sem=send_sems.at[way, step, j],
-            recv_sem=recv_sems.at[way, step, j],
+            src_ref=piece(way, step, j, part),
+            dst_ref=piece(way, step + 1, j, part),
+            send_sem=send_sems.at[way, step, j + part * blocks],
+            recv_sem=recv_sems.at[way, step, j + part * blocks],
             device_id={"tok": peers[way]},
             device_id_type=MESH,
         )
 
     def advance(way, step, j):
         term = product(home(way, step), j)
-        copy(way, step - 1, j).wait_recv()
-        here = block(way, step, j)
-        here[...] = (here[...].astype(jnp.float32) + term).astype(here.dtype)
-        copy(way, step, j).start()
+        for part in parts(j):
+            copy(way, step - 1, j, part).wait_recv()
+            here = piece(way, step, j, part)
+            rows = here.shape[0]
+            mine_here = term[part * rows : (part + 1) * rows]
+            here[...] = (here[...].astype(jnp.float32) + mine_here).astype(here.dtype)
+            copy(way, step, j, part).start()
 
     kept, cand = range(kshare), range(kshare, blocks)
 
@@ -270,7 +281,8 @@
                 here[...] = product(home(way, 0), j).astype(here.dtype)
         for j in js:
             for way in range(2):
-                copy(way, 0, j).start()
+                for part in parts(j):
+                    copy(way, 0, j, part).start()
 
     def both(step, js):
         for j in js:
@@ -280,7 +292,8 @@
     def total(j):
         value = product(t, j)
         for way in (1, 0):
-            copy(way, hops[way] - 1, j).wait_recv()
+            for part in parts(j):
+                copy(way, hops[way] - 1, j, part).wait_recv()
             value = value + block(way, hops[way], j)[...].astype(jnp.float32)
         return value
 
@@ -331,13 +344,15 @@
     def sent(step, carry):
         for way in range(2):
             for j in range(blocks):
-                copy(way, step, j).wait_send()
+                for part in parts(j):
+                    copy(way, step, j, part).wait_send()
         return carry
 
     lax.fori_loop(0, down_hops, sent, 0)
     for step in range(down_hops, up_hops):
         for j in range(blocks):
-            copy(0, step, j).wait_send()
+            for part in parts(j):
+                copy(0, step, j, part).wait_send()
     finish()
     score_ref[...] = norms / (jnp.max(plane[...]) + 1e-06)
 
@@ -388,8 +403,8 @@
             pltpu.VMEM((width, tokens, BLOCK), outgoing.dtype),
             pltpu.VMEM((2, steps + 1, kshare, BLOCK, BLOCK), jnp.float32),
             pltpu.VMEM((2, steps + 1, share, BLOCK, BLOCK), jnp.bfloat16),
-            dma((2, steps, kshare + share)),
-            dma((2, steps, kshare + share)),
+            dma((2, steps, 2 * kshare + share)),
+            dma((2, steps, 2 * kshare + share)),
             pltpu.VMEM((1, BLOCK), jnp.float32),
             pltpu.VMEM((1, BLOCK), jnp.float32),
             pltpu.VMEM((toks, 1, BLOCK), jnp.float32),

time: 97.9 us -> 97.2 us (level)
  no operation moved by 1% of the time
where the time goes in v7:
time: 97.2 us; the launch traced here: 96.9 us
  Pallas kernels  88.9 us (91%)
  other arithmetic  4.02 us (4%)
  local copies, waits for them, and re-layouts  3.29 us (3%)
    pallas_call x1, Pallas kernels, local(): pl.pallas_call(update_kernel, out_shape=(jax.ShapeDtypeStruct((kshare, BL...  86.2 us
    pallas_call x1, Pallas kernels, local(): pl.pallas_call(lambda *refs: pick_kernel(owners, width, *refs), out_shape...  2.7 us
    unnamed x9, local copies, waits for them, and re-layouts  2.63 us

profile of v7, /device:TPU:1, one launch (start us, length us, event | category | flops | bytes accessed | tf_op | source)
XLA Modules:
  0.0 96.9 jit_solution(3917686795745099981)
XLA Ops:
  0.6 0.0 copy-start.1
  0.6 0.0 copy-start
  0.7 0.7 copy-done.1
  1.3 0.1 copy.8
  1.4 0.0 copy-done
  1.4 0.1 broadcast_compare_fusion
  1.5 0.1 add_select_fusion
  1.6 0.9 fusion
  2.6 0.6 select_reduce_fusion.1
  3.2 0.6 select_reduce_fusion.2
  3.8 1.0 select_reduce_fusion
  4.8 0.7 fusion.3
  5.4 0.7 reshape.63.refs_0_
  6.1 2.7 %pick.1.out_ref = bf16[32,4,2048]{2,1,0:T(4,128)(2,1)} custom-call(s32[512]{0:T(512)} %reshape.63.refs_0_, bf16[4,29568]{1,0:T(4,128)(2,1)} %refs_1_.1), custom_call_target="tpu_custom_call" | custom-call | tf_op jit(solution)/shard_map/pick/pallas_call | solution.py:371
  8.8 86.2 %update.1 = (bf16[1,128,128]{2,1,0:T(8,128)(2,1)}, f32[1,128]{1,0:T(1,128)}) custom-call(s32[64]{0:T(128)} %get-tuple-element.7.row_ref, s32[64]{0:T(128)} %get-tuple-element.6.col_ref, bf16[128,256]{1,0:T(8,128)(2,1)} %acts_ref.1, bf16[32,4,2048]{2,1,0:T(4,128)(2,1)} %pick.1.out_ref), custom_call_target="tpu_custom_call" | custom-call | tf_op jit(solution)/shard_map/update/pallas_call | solution.py:385
  95.0 0.0 copy-start.2
  95.0 1.4 %copy.11 = bf16[1,1,128,128]{3,2,1,0:T(8,128)(2,1)} copy(bf16[1,1,128,128]{3,2,1,0:T(8,128)(2,1)} %bitcast.6) | data formatting | bytes 65536
  96.4 0.0 copy-done.2
  96.4 0.5 copy.12
  (2 shorter events, 0.0 us)
Async XLA Ops:
  0.6 0.7 copy-start.1
  0.6 0.8 copy-start
  95.0 1.4 %copy-start.2 = (f32[1,128]{1,0:T(1,128)S(1)}, f32[1,128]{1,0:T(1,128)}, u32[]{:S(2)}) copy-start(f32[1,128]{1,0:T(1,128)} %get-tuple-element.5) | copy-start | bytes 1540

commit v8 on v7

--- a/solution.py
+++ b/solution.py
@@ -166,10 +166,10 @@
 
     for h in range(2):
         forward(h, 0, 0)
+    lax.fori_loop(1, nb, start_grad, 0)
     for i, j in ((1, 0), (3, 0), (0, 1), (0, 3)):
         for h in range(2):
             arrive(h, i, j)
-    lax.fori_loop(1, nb, start_grad, 0)
     own_acts = [
         pltpu.make_async_copy(halves[h], all_ref.at[b * per + h], own_sem.at[h]) for h in range(2)
     ]

time: 97.2 us -> 97 us (level)
  no operation moved by 1% of the time
where the time goes in v8:
time: 97 us; the launch traced here: 96.7 us
  Pallas kernels  88.7 us (91%)
  other arithmetic  4.02 us (4%)
  local copies, waits for them, and re-layouts  3.29 us (3%)
    pallas_call x1, Pallas kernels, local(): pl.pallas_call(update_kernel, out_shape=(jax.ShapeDtypeStruct((kshare, BL...  86 us
    pallas_call x1, Pallas kernels, local(): pl.pallas_call(lambda *refs: pick_kernel(owners, width, *refs), out_shape...  2.7 us
    unnamed x9, local copies, waits for them, and re-layouts  2.63 us

profile of v8, /device:TPU:1, one launch (start us, length us, event | category | flops | bytes accessed | tf_op | source)
XLA Modules:
  0.0 96.7 jit_solution(2245427831065592605)
XLA Ops:
  0.6 0.0 copy-start.1
  0.6 0.0 copy-start
  0.7 0.7 copy-done.1
  1.3 0.1 copy.8
  1.4 0.0 copy-done
  1.4 0.1 broadcast_compare_fusion
  1.5 0.1 add_select_fusion
  1.6 0.9 fusion
  2.6 0.6 select_reduce_fusion.1
  3.2 0.6 select_reduce_fusion.2
  3.8 1.0 select_reduce_fusion
  4.8 0.7 fusion.3
  5.4 0.7 reshape.63.refs_0_
  6.1 2.7 %pick.1.out_ref = bf16[32,4,2048]{2,1,0:T(4,128)(2,1)} custom-call(s32[512]{0:T(512)} %reshape.63.refs_0_, bf16[4,29568]{1,0:T(4,128)(2,1)} %refs_1_.1), custom_call_target="tpu_custom_call" | custom-call | tf_op jit(solution)/shard_map/pick/pallas_call | solution.py:371
  8.8 86.0 %update.1 = (bf16[1,128,128]{2,1,0:T(8,128)(2,1)}, f32[1,128]{1,0:T(1,128)}) custom-call(s32[64]{0:T(128)} %get-tuple-element.7.row_ref, s32[64]{0:T(128)} %get-tuple-element.6.col_ref, bf16[128,256]{1,0:T(8,128)(2,1)} %acts_ref.1, bf16[32,4,2048]{2,1,0:T(4,128)(2,1)} %pick.1.out_ref), custom_call_target="tpu_custom_call" | custom-call | tf_op jit(solution)/shard_map/update/pallas_call | solution.py:385
  94.8 0.0 copy-start.2
  94.8 1.4 %copy.11 = bf16[1,1,128,128]{3,2,1,0:T(8,128)(2,1)} copy(bf16[1,1,128,128]{3,2,1,0:T(8,128)(2,1)} %bitcast.6) | data formatting | bytes 65536
  96.2 0.0 copy-done.2
  96.2 0.5 copy.12
  (2 shorter events, 0.0 us)
Async XLA Ops:
  0.6 0.7 copy-start.1
  0.6 0.8 copy-start
  94.8 1.4 %copy-start.2 = (f32[1,128]{1,0:T(1,128)S(1)}, f32[1,128]{1,0:T(1,128)}, u32[]{:S(2)}) copy-start(f32[1,128]{1,0:T(1,128)} %get-tuple-element.5) | copy-start | bytes 1540
